TPU v7x, 256 devices: a whole 4x4x8 slice. The times are simulated.
256 devices in a mesh: patch: 32 (over z, y_lo, core), lev: 8 (over y_hi, x).
Axes of the slice: x: 4, y: 4 (y_hi: 2, y_lo: 2; y = y_hi * 2 + y_lo), z: 8, core: 2. Of those that a mesh axis runs over, the one named last changes fastest.
Arguments:
- fields: float32 [3, 96, 65536], P(None, 'lev', 'patch'), may hold values from -6 to 6
- stencil_index: int32 [12, 8, 65536], P(None, 'lev', 'patch'), may hold values from 0 to 3071, as said below
- stencil_weight: float32 [12, 8, 65536], P(None, 'lev', 'patch'), may hold values from -0.2 to 0.4
- neighbours: int32 [6, 65536], P(None, 'patch'), may hold values from 0 to 2175, as said below
- lap_weight: float32 [6, 65536], P(None, 'patch'), may hold values from 0.2 to 1
- edge_x: float32 [6, 65536], P(None, 'patch'), may hold values from -1.8 to 1.8
- edge_y: float32 [6, 65536], P(None, 'patch'), may hold values from -1.8 to 1.8
- to_modes: float32 [96, 96], replicated, may hold values from -0.625 to 0.625
- from_modes: float32 [96, 96], replicated, may hold values from -0.625 to 0.625
- helm_coef: float32 [96], P('lev'), may hold values from 0.15 to 0.6
Outputs:
- new_winds: float32 [2, 96, 65536], P(None, 'lev', 'patch')
- new_height: float32 [96, 65536], P('lev', 'patch')
Inputs may be any that keep to these rules, and one draw needn't show every extreme that they name: `stencil_index`: entry [p, g, i] is a position in the cells of i's patch extended by 512 cells on each side along the closed chain; position 512 + (i mod 2048) is cell i itself, and the entry lies at most 512 from it. `neighbours`: entry [k, i] is a position in the cells of i's patch extended by 64 cells on each side along the closed chain; position 64 + (i mod 2048) is cell i itself, which is never named.
All inputs are finite; a program needn't handle non-finite values.
Results may differ from a plain program's by a relative error of at most 0.000096.
Values sent between devices are 32-bit elements; how exact they have to be, the bound alone decides.
No kernel may reach another device: no remote copies, remote signals or barrier semaphores. Data moves between devices by JAX's collectives and lax.ppermute only.
A program may use at most 64 MiB of HBM per device.

v0:
```python
import math

import jax
import jax.numpy as jnp
from jax import lax
from jax.sharding import PartitionSpec as P

REACH = 512
NBR_REACH = 64
SWEEPS = 4


coupling = 0.5


def extended_2(cells, sides, width):
    for axis, dim in sides:
        count = lax.axis_size(axis)
        head = lax.slice_in_dim(cells, 0, width, axis=dim)
        tail = lax.slice_in_dim(cells, cells.shape[dim] - width, cells.shape[dim], axis=dim)
        cells = jnp.concatenate(
            [
                lax.ppermute(tail, axis, [(i, (i + 1) % count) for i in range(count)]),
                cells,
                lax.ppermute(head, axis, [((i + 1) % count, i) for i in range(count)]),
            ],
            axis=dim,
        )
    return cells


def in_blocks(x, dim, size):
    dims = x.shape
    parts = x.reshape(*dims[:dim], size, dims[dim] // size, *dims[dim + 1 :])
    return jnp.moveaxis(parts, dim, 0)


def sent_and_summed(x, axis, dim):
    parts = in_blocks(x, dim, lax.axis_size(axis))
    arrived = lax.all_to_all(parts, axis, split_axis=0, concat_axis=0, tiled=True)
    return arrived.sum(axis=0)


def sent_to_all(x, axis):
    copies = jnp.broadcast_to(x, (lax.axis_size(axis), *x.shape))
    return lax.all_to_all(copies, axis, split_axis=0, concat_axis=0, tiled=True)


def in_order(parts, dim):
    parts = jnp.moveaxis(parts, 0, dim)
    dims = parts.shape
    return parts.reshape(*dims[:dim], dims[dim] * dims[dim + 1], *dims[dim + 2 :])


def gather_directly(x, axis, dim):
    parts = sent_to_all(x, axis)
    return in_order(parts, dim)


def block_size(cell_count, rim_width):
    return math.gcd(math.gcd(cell_count, rim_width), 128)


def band_matrix(positions, coefs, rim_width):
    cell_count = positions.shape[-1]
    block = block_size(cell_count, rim_width)
    blocks = cell_count // block
    window = block + rim_width
    offsets = (jnp.arange(blocks, dtype=jnp.int32) * block)[:, None]
    slots = jnp.arange(window, dtype=jnp.int32)[None, :, None]
    matrix = jnp.zeros((blocks, window, block), jnp.float32)
    for point_no in range(positions.shape[0]):
        local = (positions[point_no].reshape(blocks, block) - offsets)[:, None, :]
        weight = coefs[point_no].reshape(blocks, block)[:, None, :]
        matrix = matrix + jnp.where(local == slots, weight, 0.0)
    return matrix


def band_apply(extended, matrix):
    blocks, window, block = matrix.shape
    rim_width = window - block
    lead = extended.shape[:-1]
    pieces = extended.reshape(lead + (extended.shape[-1] // block, block))
    parts = [
        pieces[..., part_no : part_no + blocks, :] for part_no in range(rim_width // block + 1)
    ]
    windows = jnp.concatenate(parts, axis=-1)
    result = jnp.einsum("...ke,kec->...kc", windows, matrix, precision=lax.Precision.HIGHEST)
    return result.reshape(lead + (blocks * block,))


def block_rim(iterate):
    return extended_2(iterate, (("patch", 1),), NBR_REACH)


def chebyshev(modal_rhs, coefs, nbr_local, weights, extend):
    lap_matrix = band_matrix(nbr_local, weights, 2 * NBR_REACH)
    stiffness = coefs[:, None]
    weight_sum = jnp.sum(weights, axis=0)
    diagonal = 1.0 + stiffness * weight_sum[None, :]
    radius = 6.0 * stiffness / (1.0 + 6.0 * stiffness)
    first_step = 1.0 / (1.0 + radius * jnp.cos(jnp.pi / (2.0 * SWEEPS)))
    iterate = first_step * modal_rhs / diagonal
    for sweep_no in range(1, SWEEPS):
        step_size = 1.0 / (1.0 + radius * jnp.cos(jnp.pi * (2 * sweep_no + 1) / (2.0 * SWEEPS)))
        iter_ext = extend(iterate)
        laplace = band_apply(iter_ext, lap_matrix) - weight_sum[None, :] * iterate
        applied = iterate - stiffness * laplace
        iterate = iterate + step_size * (modal_rhs - applied) / diagonal
    return iterate


def per_device(
    fields,
    stencil_index,
    stencil_weight,
    neighbours,
    lap_weight,
    edge_x,
    edge_y,
    to_modes,
    from_modes,
    helm_coef,
):
    group_rows = fields.shape[1]
    level_index = lax.axis_index("lev")
    extended = extended_2(fields, (("patch", 2),), REACH)
    sl_matrix = band_matrix(stencil_index[:, 0, :], stencil_weight[:, 0, :], 2 * REACH)
    upstream = band_apply(extended, sl_matrix)
    new_winds = upstream[0:2]
    wind_ext = extended_2(new_winds, (("patch", 2),), NBR_REACH)
    x_matrix = band_matrix(neighbours, edge_x, 2 * NBR_REACH)
    y_matrix = band_matrix(neighbours, edge_y, 2 * NBR_REACH)
    across = band_apply(wind_ext[0], x_matrix) - jnp.sum(edge_x, axis=0)[None, :] * new_winds[0]
    along = band_apply(wind_ext[1], y_matrix) - jnp.sum(edge_y, axis=0)[None, :] * new_winds[1]
    right_side = upstream[2] - coupling * (across + along)
    own_columns = lax.dynamic_slice_in_dim(to_modes, level_index * group_rows, group_rows, 1)
    modal_rhs = sent_and_summed(
        jnp.dot(
            own_columns,
            right_side,
            precision=lax.Precision.HIGHEST,
            preferred_element_type=jnp.float32,
        ),
        "lev",
        0,
    )
    iterate = chebyshev(modal_rhs, helm_coef, neighbours, lap_weight, block_rim)
    own_rows = lax.dynamic_slice_in_dim(from_modes, level_index * group_rows, group_rows, 0)
    new_height = jnp.dot(
        own_rows,
        gather_directly(iterate, "lev", 0),
        precision=lax.Precision.HIGHEST,
        preferred_element_type=jnp.float32,
    )
    return (new_winds, new_height)


def solution(mesh):
    in_specs = (
        P(None, "lev", "patch"),
        P(None, "lev", "patch"),
        P(None, "lev", "patch"),
        P(None, "patch"),
        P(None, "patch"),
        P(None, "patch"),
        P(None, "patch"),
        P(),
        P(),
        P("lev"),
    )
    out_specs = (P(None, "lev", "patch"), P("lev", "patch"))
    return jax.shard_map(
        per_device, mesh=mesh, in_specs=in_specs, out_specs=out_specs, check_vma=False
    )
```

profile of v0, /device:TPU:105, one launch (start us, length us, event | category | flops | bytes accessed | tf_op | source)
XLA Modules:
  0.0 116.7 jit_solution(15381495268820525941)
XLA Ops:
  0.6 1.0 fusion.155
  1.6 0.8 collective-permute-start.1
  2.4 3.2 %collective-permute-start = (f32[3,12,512]{2,1,0:T(8,128)S(1)}, f32[3,12,512]{2,1,0:T(8,128)S(1)}, u32[]{:S(2)}, u32[]{:S(2)}) collective-permute-start(f32[3,12,512]{2,1,0:T(8,128)S(1)} %get-tuple-element.15), channel_id=1, source_target_pairs={{0,8},{8,16},{16,24},{24,32},{32,40},{40,48},{48,56},{56,64},{64,7... | collective-permute-start | bytes 221192 | tf_op jit(solution)/shard_map/ppermute | solution.py:23
  5.6 0.9 fusion.166
  6.4 1.1 fusion.169
  7.6 0.9 fusion.165
  8.4 1.1 fusion.170
  9.6 1.1 fusion.168
  10.7 0.1 broadcast_subtract_fusion.5
  10.8 1.0 pad_maximum_fusion
  11.9 0.3 fusion.154
  12.2 0.1 copy_dynamic-update-slice_fusion.8
  12.3 0.1 copy_dynamic-update-slice_fusion.7
  13.2 20.4 %fusion.74 = f32[3,12,16,128]{3,1,0,2:T(8,128)S(1)} fusion(f32[3,12,16,1152]{3,1,0,2:T(8,128)S(1)} %copy_dynamic-update-slice_fusion, f32[16,128]{1,0:T(8,128)S(1)} %bitcast.148, s32[16,128]{1,0:T(8,128)S(1)} %get-tuple-element.97, f32[16,128]{1,0:T(8,128)S(1)} %bitcast.149, s32[16,128]{1,0:T(8,128)S(1)} %get-tuple-element.96, f32[16,128]{1,0:T(8,128)S(1)} %bitcast.139, ...), kind=kOutput, calls=%fused_computation.93 | convolution fusion | flops 1101791232 | bytes 3145728 | tf_op jit(solution)/shard_map/...ke,kec->...kc/dot_general | solution.py:88
  33.6 0.1 copy.21
  33.7 0.1 slice.329
  33.9 0.9 collective-permute-start.2
  35.0 0.7 collective-permute-done.2
  35.6 4.4 %collective-permute-done.3 = f32[2,12,64]{2,0,1:T(2,128)S(1)} collective-permute-done((f32[2,12,64]{2,0,1:T(2,128)S(1)}, f32[2,12,64]{2,0,1:T(2,128)S(1)}, u32[]{:S(2)}, u32[]{:S(2)}) %collective-permute-start.3) | collective-permute-done | bytes 6176 | tf_op jit(solution)/shard_map/ppermute | solution.py:25
  40.0 0.4 concatenate.35
  40.5 0.5 slice_reduce_fusion
  41.3 2.8 %fusion.95 = f32[1,12,16,128]{3,1,0,2:T(8,128)S(1)} fusion(f32[16,128]{1,0:T(8,128)S(1)} %bitcast.137, s32[16,128]{1,0:T(8,128)S(1)} %get-tuple-element.102, f32[16,128]{1,0:T(8,128)S(1)} %bitcast.133, s32[16,128]{1,0:T(8,128)S(1)} %get-tuple-element.101, f32[16,128]{1,0:T(8,128)S(1)} %bitcast.134, s32[16,128]{1,0:T(8,128)S(1)} %get-tuple-element.100, ...), kind=kOutput, calls=%fused_computation.103 | convolution fusion | flops 84508672 | bytes 499712 | tf_op jit(solution)/shard_map/...ke,kec->...kc/dot_general | solution.py:88
  44.1 2.8 %fusion.92 = f32[1,12,16,128]{3,1,0,2:T(8,128)S(1)} fusion(f32[1,12,16,128]{3,1,0,2:T(8,128)S(1)} %fusion.95, f32[16,128]{1,0:T(8,128)S(1)} %bitcast.131, f32[16,128]{1,0:T(8,128)S(1)} %bitcast.127, f32[16,128]{1,0:T(8,128)S(1)} %bitcast.128, f32[16,128]{1,0:T(8,128)S(1)} %bitcast.129, f32[16,128]{1,0:T(8,128)S(1)} %bitcast.130, ...), kind=kOutput, calls=%fused_computation.102 | convolution fusion | flops 84582400 | bytes 696320 | tf_op jit(solution)/shard_map/...ke,kec->...kc/dot_general | solution.py:88
  47.1 2.0 %fusion.171 = f32[8,12,2048]{2,1,0:T(8,128)} fusion(f32[8,12,12]{2,1,0:T(8,128)S(1)} %reshape.464, f32[12,2048,1]{1,0,2:T(8,128)S(1)} %reshape.463), kind=kOutput, calls=%fused_computation.220 | convolution fusion | flops 28311552 | bytes 889344 | tf_op jit(solution)/shard_map/dot_general | solution.py:139
  49.0 5.8 %all-to-all-start = ((f32[8,12,2048]{2,1,0:T(8,128)}), f32[8,12,2048]{2,1,0:T(8,128)S(1)}, u32[]{:S(2)}, u32[]{:S(2)}) async-start(f32[8,12,2048]{2,1,0:T(8,128)} %fusion.171), calls=%async_computation | async-start | bytes 2097152 | tf_op jit(solution)/shard_map/all_to_all | solution.py:40
  54.9 14.2 %all-to-all-done = f32[8,12,2048]{2,1,0:T(8,128)S(1)} async-done(((f32[8,12,2048]{2,1,0:T(8,128)}), f32[8,12,2048]{2,1,0:T(8,128)S(1)}, u32[]{:S(2)}, u32[]{:S(2)}) %all-to-all-start) | async-done | bytes 786464 | tf_op jit(solution)/shard_map/all_to_all | solution.py:40
  69.1 0.1 fusion.139
  69.3 3.2 %collective-permute-start.4 = (f32[12,64]{1,0:T(8,128)S(1)}, f32[12,64]{1,0:T(8,128)S(1)}, u32[]{:S(2)}, u32[]{:S(2)}) collective-permute-start(f32[12,64]{1,0:T(8,128)S(1)} %get-tuple-element.34), channel_id=1, source_target_pairs={{0,8},{8,16},{16,24},{24,32},{32,40},{40,48},{48,56},{56,64},{64,7... | collective-permute-start | bytes 9224 | tf_op jit(solution)/shard_map/ppermute | solution.py:23
  72.5 0.8 collective-permute-done.4
  73.3 4.4 %collective-permute-done.5 = f32[12,64]{1,0:T(8,128)S(1)} collective-permute-done((f32[12,64]{1,0:T(8,128)S(1)}, f32[12,64]{1,0:T(8,128)S(1)}, u32[]{:S(2)}, u32[]{:S(2)}) %collective-permute-start.5) | collective-permute-done | bytes 3104 | tf_op jit(solution)/shard_map/ppermute | solution.py:25
  77.7 0.1 concatenate.38
  77.9 2.8 %convolution_bitcast_fusion.2 = f32[12,16,128]{2,0,1:T(8,128)S(1)} fusion(f32[16,128]{1,0:T(8,128)S(1)} %bitcast.162, f32[16,128]{1,0:T(8,128)S(1)} %bitcast.165, f32[16,128]{1,0:T(8,128)S(1)} %bitcast.153, f32[16,128]{1,0:T(8,128)S(1)} %bitcast.156, f32[16,128]{1,0:T(8,128)S(1)} %bitcast.159, f32[16,128]{1,0:T(8,128)S(1)} %bitcast.150, ...), kind=kOutput, calls=%fused_computation.96 | convolution fusion | flops 84459520 | bytes 393216 | tf_op jit(solution)/shard_map/...ke,kec->...kc/dot_general | solution.py:88
  80.9 0.1 divide_add_fusion.2
  81.1 0.5 collective-permute-start.7
  81.6 0.7 collective-permute-done.6
  82.3 4.1 %collective-permute-done.7 = f32[12,64]{1,0:T(8,128)S(1)} collective-permute-done((f32[12,64]{1,0:T(8,128)S(1)}, f32[12,64]{1,0:T(8,128)S(1)}, u32[]{:S(2)}, u32[]{:S(2)}) %collective-permute-start.7) | collective-permute-done | bytes 3104 | tf_op jit(solution)/shard_map/ppermute | solution.py:25
  86.4 0.1 concatenate.40
  86.6 2.8 %convolution_bitcast_fusion.1 = f32[12,16,128]{2,0,1:T(8,128)S(1)} fusion(f32[16,128]{1,0:T(8,128)S(1)} %bitcast.163, f32[16,128]{1,0:T(8,128)S(1)} %bitcast.166, f32[16,128]{1,0:T(8,128)S(1)} %bitcast.154, f32[16,128]{1,0:T(8,128)S(1)} %bitcast.157, f32[16,128]{1,0:T(8,128)S(1)} %bitcast.160, f32[16,128]{1,0:T(8,128)S(1)} %bitcast.151, ...), kind=kOutput, calls=%fused_computation.95 | convolution fusion | flops 84459520 | bytes 393216 | tf_op jit(solution)/shard_map/...ke,kec->...kc/dot_general | solution.py:88
  89.6 0.1 divide_add_fusion.1
  89.8 0.5 collective-permute-start.9
  90.3 0.7 collective-permute-done.8
  91.0 4.4 %collective-permute-done.9 = f32[12,64]{1,0:T(8,128)S(1)} collective-permute-done((f32[12,64]{1,0:T(8,128)S(1)}, f32[12,64]{1,0:T(8,128)S(1)}, u32[]{:S(2)}, u32[]{:S(2)}) %collective-permute-start.9) | collective-permute-done | bytes 3104 | tf_op jit(solution)/shard_map/ppermute | solution.py:25
  95.3 0.1 concatenate.42
  95.6 2.8 %convolution_bitcast_fusion = f32[12,16,128]{2,0,1:T(8,128)S(1)} fusion(f32[16,128]{1,0:T(8,128)S(1)} %bitcast.164, f32[16,128]{1,0:T(8,128)S(1)} %bitcast.167, f32[16,128]{1,0:T(8,128)S(1)} %bitcast.155, f32[16,128]{1,0:T(8,128)S(1)} %bitcast.158, f32[16,128]{1,0:T(8,128)S(1)} %bitcast.161, f32[16,128]{1,0:T(8,128)S(1)} %bitcast.152, ...), kind=kOutput, calls=%fused_computation.94 | convolution fusion | flops 84459520 | bytes 393216 | tf_op jit(solution)/shard_map/...ke,kec->...kc/dot_general | solution.py:88
  98.5 0.1 divide_add_fusion
  98.6 0.1 broadcast_in_dim.362
  98.7 16.7 %all_to_all.10 = f32[8,12,2048]{2,1,0:T(8,128)S(1)} all-to-all(f32[8,12,2048]{2,1,0:T(8,128)S(1)} %broadcast_in_dim.362), channel_id=1, replica_groups=mesh['patch'=32,'lev'=8] {'lev'}, dimensions={0} | all-to-all | bytes 1572864 | tf_op jit(solution)/shard_map/all_to_all | solution.py:46
  115.5 1.2 fusion.140
  (75 shorter events, 2.4 us)
Async XLA Ops:
  0.6 114.9 %copy-start = (f32[96,96]{1,0:T(8,128)S(1)}, f32[96,96]{1,0:T(8,128)}, u32[]{:S(2)}) copy-start(f32[96,96]{1,0:T(8,128)} %param.18) | copy-start | bytes 110596
  1.6 9.2 %collective-permute-start.1 = (f32[3,12,512]{2,1,0:T(8,128)S(1)}, f32[3,12,512]{2,1,0:T(8,128)S(1)}, u32[]{:S(2)}, u32[]{:S(2)}) collective-permute-start(f32[3,12,512]{2,1,0:T(8,128)S(1)} %get-tuple-element.16), channel_id=1, source_target_pairs={{8,0},{16,8},{24,16},{32,24},{40,32},{48,40},{56,48},{64,56},{72,6... | collective-permute-start | bytes 221192 | tf_op jit(solution)/shard_map/ppermute | solution.py:25
  2.4 8.5 %collective-permute-start = (f32[3,12,512]{2,1,0:T(8,128)S(1)}, f32[3,12,512]{2,1,0:T(8,128)S(1)}, u32[]{:S(2)}, u32[]{:S(2)}) collective-permute-start(f32[3,12,512]{2,1,0:T(8,128)S(1)} %get-tuple-element.15), channel_id=1, source_target_pairs={{0,8},{8,16},{16,24},{24,32},{32,40},{40,48},{48,56},{56,64},{64,7... | collective-permute-start | bytes 221192 | tf_op jit(solution)/shard_map/ppermute | solution.py:23
  13.1 21.7 %copy-start.5 = (f32[96,96]{1,0:T(8,128)S(1)}, f32[96,96]{1,0:T(8,128)}, u32[]{:S(2)}) copy-start(f32[96,96]{1,0:T(8,128)} %param.17) | copy-start | bytes 110596
  13.1 21.7 %copy-start.2 = (f32[6,2048]{1,0:T(8,128)S(1)}, f32[6,2048]{1,0:T(8,128)}, u32[]{:S(2)}) copy-start(f32[6,2048]{1,0:T(8,128)} %param.15) | copy-start | bytes 147460
  13.1 21.8 %copy-start.3 = (f32[6,2048]{1,0:T(8,128)S(1)}, f32[6,2048]{1,0:T(8,128)}, u32[]{:S(2)}) copy-start(f32[6,2048]{1,0:T(8,128)} %param.16) | copy-start | bytes 147460
  33.8 10.3 %copy-start.1 = (f32[2,12,2048]{2,0,1:T(2,128)}, f32[2,12,2048]{2,0,1:T(2,128)S(1)}, u32[]{:S(2)}) copy-start(f32[2,12,2048]{2,0,1:T(2,128)S(1)} %slice.329) | copy-start | bytes 589828
  33.9 1.7 %collective-permute-start.2 = (f32[2,12,64]{2,0,1:T(2,128)S(1)}, f32[2,12,64]{2,0,1:T(2,128)S(1)}, u32[]{:S(2)}, u32[]{:S(2)}) collective-permute-start(f32[2,12,64]{2,0,1:T(2,128)S(1)} %get-tuple-element.18), channel_id=1, source_target_pairs={{0,8},{8,16},{16,24},{24,32},{32,40},{40,48},{48,56},{56,64},{64,7... | collective-permute-start | bytes 18440 | tf_op jit(solution)/shard_map/ppermute | solution.py:23
  34.8 5.2 %collective-permute-start.3 = (f32[2,12,64]{2,0,1:T(2,128)S(1)}, f32[2,12,64]{2,0,1:T(2,128)S(1)}, u32[]{:S(2)}, u32[]{:S(2)}) collective-permute-start(f32[2,12,64]{2,0,1:T(2,128)S(1)} %get-tuple-element.17), channel_id=1, source_target_pairs={{8,0},{16,8},{24,16},{32,24},{40,32},{48,40},{56,48},{64,56},{72,6... | collective-permute-start | bytes 18440 | tf_op jit(solution)/shard_map/ppermute | solution.py:25
  47.0 7.8 %copy-start.4 = (f32[6,2048]{1,0:T(8,128)S(1)}, f32[6,2048]{1,0:T(8,128)}, u32[]{:S(2)}) copy-start(f32[6,2048]{1,0:T(8,128)} %param.14) | copy-start | bytes 147460
  47.0 7.8 %copy-start.6 = (f32[12]{0:T(128)S(1)}, f32[12]{0:T(128)}, u32[]{:S(2)}) copy-start(f32[12]{0:T(128)} %param.19) | copy-start | bytes 148
  49.0 20.0 %all-to-all-start = ((f32[8,12,2048]{2,1,0:T(8,128)}), f32[8,12,2048]{2,1,0:T(8,128)S(1)}, u32[]{:S(2)}, u32[]{:S(2)}) async-start(f32[8,12,2048]{2,1,0:T(8,128)} %fusion.171), calls=%async_computation | async-start | bytes 2097152 | tf_op jit(solution)/shard_map/all_to_all | solution.py:40
  69.3 4.0 %collective-permute-start.4 = (f32[12,64]{1,0:T(8,128)S(1)}, f32[12,64]{1,0:T(8,128)S(1)}, u32[]{:S(2)}, u32[]{:S(2)}) collective-permute-start(f32[12,64]{1,0:T(8,128)S(1)} %get-tuple-element.34), channel_id=1, source_target_pairs={{0,8},{8,16},{16,24},{24,32},{32,40},{40,48},{48,56},{56,64},{64,7... | collective-permute-start | bytes 9224 | tf_op jit(solution)/shard_map/ppermute | solution.py:23
  72.5 5.2 %collective-permute-start.5 = (f32[12,64]{1,0:T(8,128)S(1)}, f32[12,64]{1,0:T(8,128)S(1)}, u32[]{:S(2)}, u32[]{:S(2)}) collective-permute-start(f32[12,64]{1,0:T(8,128)S(1)} %get-tuple-element.33), channel_id=1, source_target_pairs={{8,0},{16,8},{24,16},{32,24},{40,32},{48,40},{56,48},{64,56},{72,6... | collective-permute-start | bytes 9224 | tf_op jit(solution)/shard_map/ppermute | solution.py:25
  81.1 1.2 %collective-permute-start.6 = (f32[12,64]{1,0:T(8,128)S(1)}, f32[12,64]{1,0:T(8,128)S(1)}, u32[]{:S(2)}, u32[]{:S(2)}) collective-permute-start(f32[12,64]{1,0:T(8,128)S(1)} %get-tuple-element.32), channel_id=1, source_target_pairs={{0,8},{8,16},{16,24},{24,32},{32,40},{40,48},{48,56},{56,64},{64,7... | collective-permute-start | bytes 9224 | tf_op jit(solution)/shard_map/ppermute | solution.py:23
  81.1 5.2 %collective-permute-start.7 = (f32[12,64]{1,0:T(8,128)S(1)}, f32[12,64]{1,0:T(8,128)S(1)}, u32[]{:S(2)}, u32[]{:S(2)}) collective-permute-start(f32[12,64]{1,0:T(8,128)S(1)} %get-tuple-element.31), channel_id=1, source_target_pairs={{8,0},{16,8},{24,16},{32,24},{40,32},{48,40},{56,48},{64,56},{72,6... | collective-permute-start | bytes 9224 | tf_op jit(solution)/shard_map/ppermute | solution.py:25
  89.8 1.2 %collective-permute-start.8 = (f32[12,64]{1,0:T(8,128)S(1)}, f32[12,64]{1,0:T(8,128)S(1)}, u32[]{:S(2)}, u32[]{:S(2)}) collective-permute-start(f32[12,64]{1,0:T(8,128)S(1)} %get-tuple-element.30), channel_id=1, source_target_pairs={{0,8},{8,16},{16,24},{24,32},{32,40},{40,48},{48,56},{56,64},{64,7... | collective-permute-start | bytes 9224 | tf_op jit(solution)/shard_map/ppermute | solution.py:23
  89.8 5.5 %collective-permute-start.9 = (f32[12,64]{1,0:T(8,128)S(1)}, f32[12,64]{1,0:T(8,128)S(1)}, u32[]{:S(2)}, u32[]{:S(2)}) collective-permute-start(f32[12,64]{1,0:T(8,128)S(1)} %get-tuple-element.29), channel_id=1, source_target_pairs={{8,0},{16,8},{24,16},{32,24},{40,32},{48,40},{56,48},{64,56},{72,6... | collective-permute-start | bytes 9224 | tf_op jit(solution)/shard_map/ppermute | solution.py:25
where the time goes:
time: 117 us
  matrix products  37.6 us (32%)
  waiting for transfers between devices  34.2 us (29%)
  blocking collectives  16.7 us (14%)
  starting transfers between devices  14.8 us (13%)
  local copies, waits for them, and re-layouts  10.3 us (9%)
  other arithmetic  1.76 us (2%)
  between operations  1.24 us (1%)
    dot_general x6, matrix products, band_apply(): jnp.einsum('...ke,kec->...kc', windows, matrix, precision=lax.Precision.H...  34.5 us
    ppermute x5, waiting for transfers between devices, extended_2(): lax.ppermute(head, axis, [((i + 1) % count, i) for i in range(count)])  17.3 us
    all_to_all x1, blocking collectives, sent_to_all(): return lax.all_to_all(copies, axis, split_axis=0, concat_axis=0, tiled=True)  16.7 us
    all_to_all x1, waiting for transfers between devices, sent_and_summed(): lax.all_to_all(parts, axis, split_axis=0, concat_axis=0, tiled=True)  14.2 us
    ppermute x5, starting transfers between devices, extended_2(): lax.ppermute(tail, axis, [(i, (i + 1) % count) for i in range(count)])  7.39 us
    all_to_all x1, starting transfers between devices, sent_and_summed(): lax.all_to_all(parts, axis, split_axis=0, concat_axis=0, tiled=True)  5.76 us
    slice x4, local copies, waits for them, and re-layouts, band_matrix(): weight = coefs[point_no].reshape(blocks, block)[:, None, :]  3.17 us
    ppermute x5, waiting for transfers between devices, extended_2(): lax.ppermute(tail, axis, [(i, (i + 1) % count) for i in range(count)])  2.73 us
  transfers between devices with their start and end apart: 11, of which 9 were waited for; matrix products, arithmetic and copies ran while one was open for 5% of the time, Pallas kernels for 0%

commit v1 on v0

v1 whole, which is shorter than its diff:
```python
import functools
import math

import jax
import jax.numpy as jnp
from jax import lax
from jax.experimental import pallas as pl
from jax.experimental.pallas import tpu as pltpu
from jax.sharding import PartitionSpec as P

CELLS = 2048
REACH = 512
NBR_REACH = 64
SWEEPS = 4
POINTS = 12
SIDES = 6
GROUPS = 8
ROWS = 12
SLAB = 16
LANES = 128
EDGE = 256
FIELD_EDGE = EDGE + REACH
WIDE = CELLS + 2 * EDGE
WIDE_BLOCKS = WIDE // LANES
CHUNK = CELLS // GROUPS
WINDOW = CHUNK + 2 * EDGE
TILES = 9
INNER_LO = FIELD_EDGE // LANES
INNER = (CELLS - 2 * REACH) // LANES
HALO_ROWS = 56
COUPLING = 0.5

f32 = jnp.float32
bf16 = jnp.bfloat16


def pack_fields(dst, dst_col, src, src_col, count):
    d = slice(dst_col, dst_col + count)
    s = slice(src_col, src_col + count)
    for field in range(3):
        dst[8 * field : 8 * field + 8, d] = src[field, 0:8, s]
        dst[24 + 4 * field : 28 + 4 * field, d] = src[field, 8:12, s]
    dst[36:40, d] = jnp.zeros((4, count), f32)


def halo_kernel(*refs):
    group, coef, *sources = refs[:9]
    head, tail, coef_row = refs[9:12]
    buffers, coef_here, sems = refs[12:26], refs[26], refs[27]
    copies = []
    for side, (field_col, col) in enumerate(((0, 0), (CELLS - FIELD_EDGE, CELLS - EDGE))):
        for n, source in enumerate(sources):
            cells = pl.ds(field_col, FIELD_EDGE) if n == 0 else pl.ds(col, EDGE)
            part = source.at[:, cells] if n > 2 else source.at[:, :, cells]
            copies.append(pltpu.make_async_copy(part, buffers[7 * side + n], sems.at[7 * side + n]))
    copies.append(pltpu.make_async_copy(coef, coef_here, sems.at[14]))
    for copy in copies:
        copy.start()
    for side, (out, col) in enumerate(((head, 0), (tail, CELLS - EDGE))):
        for copy in copies[7 * side : 7 * side + 7]:
            copy.wait()
        fields, index, weight, nbr, lap, ex, ey = buffers[7 * side : 7 * side + 7]
        pack_fields(out, 0, fields, 0, FIELD_EDGE)
        own = col + lax.broadcasted_iota(jnp.int32, (1, EDGE), 1)
        for p in range(POINTS):
            out[40 + p : 41 + p, 0:EDGE] = (index[p] - REACH - own).astype(f32)
            out[40 + p : 41 + p, EDGE : 2 * EDGE] = weight[p]
        away = (nbr[...] - NBR_REACH - own).astype(f32)
        out[52:56, 0:EDGE] = away[0:4]
        out[52:56, EDGE : 2 * EDGE] = lap[0:4]
        out[40:46, 2 * EDGE :] = ex[...]
        out[46:52, 2 * EDGE :] = ey[...]
        out[52:54, 2 * EDGE :] = away[4:6]
        out[54:56, 2 * EDGE :] = lap[4:6]
    copies[14].wait()
    lane = lax.broadcasted_iota(jnp.int32, (1, LANES), 1)
    row = jnp.zeros((1, LANES), f32)
    for k in range(ROWS):
        row = jnp.where(lane == group[0] * ROWS + k, coef_here[k], row)
    coef_row[...] = row


def stencil_block(x, col, away, weight, away_col):
    groups = 5
    acc = [jnp.zeros((8, LANES), f32) for _ in range(groups)]
    lane = lax.broadcasted_iota(jnp.int32, (1, LANES), 1)
    for p in range(POINTS):
        at = away[p, :, pl.ds(away_col, LANES)] + (lane + REACH)
        at = jnp.broadcast_to(at, (8, LANES))
        w = jnp.broadcast_to(weight[p, :, pl.ds(away_col, LANES)], (8, LANES))
        inside = at & (LANES - 1)
        tile = at >> 7
        picked = [None] * groups
        for t in range(TILES):
            mask = tile == t
            for g in range(groups):
                part = x[8 * g : 8 * g + 8, pl.ds(col + t * LANES, LANES)]
                part = jnp.take_along_axis(part, inside, axis=1, mode="promise_in_bounds")
                picked[g] = part if t == 0 else jnp.where(mask, part, picked[g])
        for g in range(groups):
            acc[g] = acc[g] + w * picked[g]
    return acc


def inner_kernel(fields, index, weight, coef_row, packed, upstream, away):
    pack_fields(packed, 0, fields, 0, CELLS)
    packed[36:37, 0:LANES] = coef_row[...]
    own = lax.broadcasted_iota(jnp.int32, (1, CELLS), 1)
    for p in range(POINTS):
        away[p] = index[p] - REACH - own

    def body(b, carry):
        col = pl.multiple_of(b * LANES, LANES)
        acc = stencil_block(packed, col, away, weight, pl.multiple_of(col + REACH, LANES))
        for g in range(5):
            upstream[8 * g : 8 * g + 8, pl.ds(col, LANES)] = acc[g]
        return carry

    lax.fori_loop(0, INNER, body, 0)


def outer_kernel(
    packed, inner, left, right, index, weight, nbr, ex, ey,
    winds, send, x, up, away, w_all, side, side_x, side_y, rs,
):
    x[:, 0:FIELD_EDGE] = left[0:40, :]
    x[:, FIELD_EDGE : FIELD_EDGE + CELLS] = packed[...]
    x[:, FIELD_EDGE + CELLS :] = right[0:40, :]
    own = lax.broadcasted_iota(jnp.int32, (1, CELLS), 1)
    mid = slice(EDGE, EDGE + CELLS)
    for halo, cells in ((left, slice(0, EDGE)), (right, slice(EDGE + CELLS, WIDE))):
        for p in range(POINTS):
            away[p, :, cells] = halo[40 + p : 41 + p, 0:EDGE].astype(jnp.int32)
            w_all[p, :, cells] = halo[40 + p : 41 + p, EDGE : 2 * EDGE]
        side[0:4, cells] = halo[52:56, 0:EDGE].astype(jnp.int32)
        side[4:6, cells] = halo[52:54, 2 * EDGE :].astype(jnp.int32)
        side_x[:, cells] = halo[40:46, 2 * EDGE :]
        side_y[:, cells] = halo[46:52, 2 * EDGE :]
    for p in range(POINTS):
        away[p, :, mid] = index[p] - REACH - own
        w_all[p, :, mid] = weight[p]
    side[:, mid] = nbr[...] - NBR_REACH - own
    side_x[:, mid] = ex[...]
    side_y[:, mid] = ey[...]

    up[:, 0:LANES] = jnp.zeros((40, LANES), f32)
    up[:, LANES + WIDE :] = jnp.zeros((40, LANES), f32)
    first = LANES * (1 + INNER_LO)
    up[:, first : first + INNER * LANES] = inner[...]

    def stencil(i, carry):
        b = jnp.where(i < INNER_LO, i, i + INNER)
        col = pl.multiple_of(b * LANES, LANES)
        acc = stencil_block(x, col, away, w_all, col)
        for g in range(5):
            up[8 * g : 8 * g + 8, pl.ds(col + LANES, LANES)] = acc[g]
        return carry

    lax.fori_loop(0, WIDE_BLOCKS - INNER, stencil, 0)

    for field in range(2):
        cells = slice(LANES + EDGE, LANES + EDGE + CELLS)
        winds[field, 0:8, :] = up[8 * field : 8 * field + 8, cells]
        winds[field, 8:12, :] = up[24 + 4 * field : 28 + 4 * field, cells]

    lane = lax.broadcasted_iota(jnp.int32, (1, LANES), 1)
    upper = lax.broadcasted_iota(jnp.int32, (8, LANES), 0) < 4

    def divergence(b, carry):
        col = pl.multiple_of(b * LANES, LANES)
        rows = (0, 8, 24)
        here = [up[r : r + 8, pl.ds(col + LANES, LANES)] for r in rows]
        acc = [jnp.zeros((8, LANES), f32) for _ in rows]
        for k in range(SIDES):
            at = jnp.broadcast_to(side[k : k + 1, pl.ds(col, LANES)] + (lane + LANES), (8, LANES))
            inside = at & (LANES - 1)
            tile = at >> 7
            wx = jnp.broadcast_to(side_x[k : k + 1, pl.ds(col, LANES)], (8, LANES))
            wy = jnp.broadcast_to(side_y[k : k + 1, pl.ds(col, LANES)], (8, LANES))
            weights = (wx, wy, jnp.where(upper, wx, wy))
            for g, r in enumerate(rows):
                picked = None
                for t in range(3):
                    part = up[r : r + 8, pl.ds(col + t * LANES, LANES)]
                    part = jnp.take_along_axis(part, inside, axis=1, mode="promise_in_bounds")
                    picked = part if t == 0 else jnp.where(tile == t, part, picked)
                acc[g] = acc[g] + weights[g] * (picked - here[g])
        h0 = up[16:24, pl.ds(col + LANES, LANES)]
        h1 = up[32:36, pl.ds(col + LANES, LANES)]
        rs[0:8, pl.ds(col, LANES)] = h0 - COUPLING * (acc[0] + acc[1])
        rs[8:12, pl.ds(col, LANES)] = h1 - COUPLING * (acc[2][0:4] + acc[2][4:8])
        return carry

    lax.fori_loop(0, WIDE_BLOCKS, divergence, 0)

    rs[12:16, :] = jnp.zeros((4, WIDE), f32)
    for j in range(GROUPS):
        send[j] = rs[:, j * CHUNK : j * CHUNK + WINDOW]
        send[j, 12:13, 0:LANES] = packed[36:37, 0:LANES]


def split(v):
    high = v.astype(bf16)
    return high, (v - high.astype(f32)).astype(bf16)


def dot3(a, b):
    ah, al = a
    bh, bl = b
    dot = functools.partial(jnp.dot, preferred_element_type=f32)
    return dot(ah, bh) + (dot(al, bh) + dot(ah, bl))


def band_kernel(group, left, right, nbr, lap, high, low, total, side, side_w):
    own = lax.broadcasted_iota(jnp.int32, (1, CELLS), 1)
    mid = slice(EDGE, EDGE + CELLS)
    for halo, cells in ((left, slice(0, EDGE)), (right, slice(EDGE + CELLS, WIDE))):
        side[0:4, cells] = halo[52:56, 0:EDGE].astype(jnp.int32)
        side[4:6, cells] = halo[52:54, 2 * EDGE :].astype(jnp.int32)
        side_w[0:4, cells] = halo[52:56, EDGE : 2 * EDGE]
        side_w[4:6, cells] = halo[54:56, 2 * EDGE :]
    side[:, mid] = nbr[...] - NBR_REACH - own
    side_w[:, mid] = lap[...]
    start = pl.multiple_of(group[0] * CHUNK, LANES)
    total[...] = jnp.sum(side_w[:, pl.ds(start, WINDOW)], axis=0, keepdims=True)
    lane = lax.broadcasted_iota(jnp.int32, (1, LANES), 1)
    slot = lax.broadcasted_iota(jnp.int32, (3 * LANES, LANES), 0)
    for b in range(4):
        cells = pl.ds(pl.multiple_of(start + (b + 1) * LANES, LANES), LANES)
        matrix = jnp.zeros((3 * LANES, LANES), f32)
        for k in range(SIDES):
            at = side[k : k + 1, cells] + (lane + LANES)
            matrix = matrix + jnp.where(slot == at, side_w[k : k + 1, cells], 0.0)
        high[b], low[b] = split(matrix)


def solve_kernel(got, high, low, total, to_modes, from_modes, out):
    levels = got[...].reshape(GROUPS * SLAB, WINDOW)
    modes = GROUPS * ROWS
    coef_row = got[0, 12:13, 0:LANES]
    for j in range(1, GROUPS):
        coef_row = coef_row + got[j, 12:13, 0:LANES]
    eye = lax.broadcasted_iota(jnp.int32, (modes, LANES), 0) == lax.broadcasted_iota(
        jnp.int32, (modes, LANES), 1
    )
    coef = jnp.sum(jnp.where(eye, coef_row, 0.0), axis=1, keepdims=True)
    rhs = dot3(split(to_modes[...]), split(levels))
    inverse = 1.0 / (1.0 + coef * total[...])
    rhs = rhs * inverse
    scaled = coef * inverse
    radius = 6.0 * coef / (1.0 + 6.0 * coef)
    steps = [
        1.0 / (1.0 + radius * math.cos(math.pi * (2 * s + 1) / (2.0 * SWEEPS)))
        for s in range(SWEEPS)
    ]
    cols = [slice(b * LANES, (b + 1) * LANES) for b in range(6)]
    iterate = [steps[0] * rhs[:, c] for c in cols]
    for sweep, blocks in ((1, (1, 2, 3, 4)), (2, (1, 2, 3, 4)), (3, (2, 3))):
        parts = [split(v) for v in iterate]
        step = steps[sweep]
        fresh = list(iterate)
        for b in blocks:
            near = [jnp.concatenate([parts[b + o][i] for o in (-1, 0, 1)], axis=1) for i in (0, 1)]
            moved = dot3(near, (high[b - 1], low[b - 1]))
            fresh[b] = (1.0 - step) * iterate[b] + step * (
                rhs[:, cols[b]] + scaled[:, cols[b]] * moved
            )
        iterate = fresh
    solved = jnp.concatenate([iterate[2], iterate[3]], axis=1)
    height = dot3(split(from_modes[...]), split(solved))
    out[...] = height.reshape(GROUPS, SLAB, CHUNK)


def place_kernel(got, out):
    for j in range(GROUPS):
        out[:, j * CHUNK : (j + 1) * CHUNK] = got[j, 0:ROWS, :]


def call(kernel, outs, scratch=(), name=None, smem=0, n_in=0, space=pltpu.VMEM, vmem=32):
    in_specs = [pl.BlockSpec(memory_space=pltpu.SMEM)] * smem + [
        pl.BlockSpec(memory_space=space)
    ] * (n_in - smem)
    shapes = [jax.ShapeDtypeStruct(s, d) for s, d in outs]
    specs = [pl.BlockSpec(memory_space=pltpu.VMEM)] * len(outs)
    if len(outs) == 1:
        shapes, specs = shapes[0], specs[0]
    return pl.pallas_call(
        kernel,
        out_shape=shapes,
        in_specs=in_specs,
        out_specs=specs,
        scratch_shapes=list(scratch),
        name=name,
        compiler_params=pltpu.CompilerParams(vmem_limit_bytes=int(vmem * 1024 * 1024)),
    )


def per_device(
    fields,
    stencil_index,
    stencil_weight,
    neighbours,
    lap_weight,
    edge_x,
    edge_y,
    to_modes,
    from_modes,
    helm_coef,
):
    patches = lax.axis_size("patch")
    group = lax.axis_index("lev")
    halo = ((HALO_ROWS, FIELD_EDGE), f32)
    buffers = [
        pltpu.VMEM((3, ROWS, FIELD_EDGE), f32),
        pltpu.VMEM((POINTS, 1, EDGE), jnp.int32),
        pltpu.VMEM((POINTS, 1, EDGE), f32),
        pltpu.VMEM((SIDES, EDGE), jnp.int32),
    ] + [pltpu.VMEM((SIDES, EDGE), f32)] * 3
    head, tail, coef_row = call(
        halo_kernel,
        [halo, halo, ((1, LANES), f32)],
        buffers * 2 + [pltpu.SMEM((ROWS,), f32), pltpu.SemaphoreType.DMA((15,))],
        name="halo",
        smem=1,
        n_in=9,
        space=pltpu.HBM,
        vmem=62,
    )(
        group[None], helm_coef, fields, stencil_index, stencil_weight, neighbours, lap_weight,
        edge_x, edge_y,
    )
    left = lax.ppermute(tail, "patch", [(i, (i + 1) % patches) for i in range(patches)])
    right = lax.ppermute(head, "patch", [((i + 1) % patches, i) for i in range(patches)])
    packed, inner = call(
        inner_kernel,
        [((40, CELLS), f32), ((40, INNER * LANES), f32)],
        [pltpu.VMEM((POINTS, 1, CELLS), jnp.int32)],
        name="inner",
        n_in=4,
    )(fields, stencil_index, stencil_weight, coef_row)
    new_winds, send = call(
        outer_kernel,
        [((2, ROWS, CELLS), f32), ((GROUPS, SLAB, WINDOW), f32)],
        [
            pltpu.VMEM((40, CELLS + 2 * FIELD_EDGE), f32),
            pltpu.VMEM((40, WIDE + 2 * LANES), f32),
            pltpu.VMEM((POINTS, 1, WIDE), jnp.int32),
            pltpu.VMEM((POINTS, 1, WIDE), f32),
            pltpu.VMEM((SIDES, WIDE), jnp.int32),
            pltpu.VMEM((SIDES, WIDE), f32),
            pltpu.VMEM((SIDES, WIDE), f32),
            pltpu.VMEM((SLAB, WIDE), f32),
        ],
        name="outer",
        n_in=9,
    )(
        packed, inner, left, right, stencil_index, stencil_weight,
        neighbours, edge_x, edge_y,
    )
    high, low, total = call(
        band_kernel,
        [((4, 3 * LANES, LANES), bf16), ((4, 3 * LANES, LANES), bf16), ((1, WINDOW), f32)],
        [pltpu.VMEM((SIDES, WIDE), jnp.int32), pltpu.VMEM((SIDES, WIDE), f32)],
        name="band",
        smem=1,
        n_in=5,
    )(group[None], left, right, neighbours, lap_weight)
    got = lax.all_to_all(send, "lev", split_axis=0, concat_axis=0, tiled=True)
    pad = ((0, 0), (0, 0), (0, SLAB - ROWS))
    modes = GROUPS * ROWS
    to_wide = jnp.pad(to_modes.reshape(modes, GROUPS, ROWS), pad).reshape(modes, GROUPS * SLAB)
    from_wide = jnp.pad(
        from_modes.reshape(GROUPS, ROWS, modes), ((0, 0), (0, SLAB - ROWS), (0, 0))
    ).reshape(GROUPS * SLAB, modes)
    heights = call(solve_kernel, [((GROUPS, SLAB, CHUNK), f32)], name="solve", n_in=6)(
        got, high, low, total, to_wide, from_wide
    )
    heights = lax.all_to_all(heights, "lev", split_axis=0, concat_axis=0, tiled=True)
    new_height = call(place_kernel, [((ROWS, CELLS), f32)], name="place", n_in=1)(heights)
    return new_winds, new_height


def solution(mesh):
    in_specs = (
        P(None, "lev", "patch"),
        P(None, "lev", "patch"),
        P(None, "lev", "patch"),
        P(None, "patch"),
        P(None, "patch"),
        P(None, "patch"),
        P(None, "patch"),
        P(),
        P(),
        P("lev"),
    )
    out_specs = (P(None, "lev", "patch"), P("lev", "patch"))
    return jax.shard_map(
        per_device, mesh=mesh, in_specs=in_specs, out_specs=out_specs, check_vma=False
    )
```

time: 117 us -> 57.7 us (0.49)
  the two profiles are of different devices: /device:TPU:105 before, /device:TPU:2 now
where the time goes in v1:
time: 57.7 us; the launch traced here: 57.3 us
  Pallas kernels  24 us (42%)
  starting transfers between devices  18.2 us (32%)
  waiting for transfers between devices  11.6 us (20%)
  local copies, waits for them, and re-layouts  2.58 us (4%)
  between operations  0.82 us (1%)
    pallas_call x1, Pallas kernels, per_device(): call(outer_kernel, [((2, ROWS, CELLS), f32), ((GROUPS, SLAB, WINDOW), f32...  12.6 us
    all_to_all x1, starting transfers between devices, per_device(): got = lax.all_to_all(send, 'lev', split_axis=0, concat_axis=0, tiled=True)  7.3 us
    ppermute x1, starting transfers between devices, per_device(): lax.ppermute(head, 'patch', [((i + 1) % patches, i) for i in range(patche...  6.38 us
    all_to_all x1, waiting for transfers between devices, per_device(): lax.all_to_all(heights, 'lev', split_axis=0, concat_axis=0, tiled=True)  6.13 us
    pallas_call x1, Pallas kernels, per_device(): call(inner_kernel, [((40, CELLS), f32), ((40, INNER * LANES), f32)], [plt...  5.71 us
    all_to_all x1, waiting for transfers between devices, per_device(): got = lax.all_to_all(send, 'lev', split_axis=0, concat_axis=0, tiled=True)  5.5 us
    all_to_all x1, starting transfers between devices, per_device(): lax.all_to_all(heights, 'lev', split_axis=0, concat_axis=0, tiled=True)  4.44 us
    unnamed x22, local copies, waits for them, and re-layouts  2.47 us
  transfers between devices with their start and end apart: 4, of which 2 were waited for; matrix products, arithmetic and copies ran while one was open for 2% of the time, Pallas kernels for 12%

profile of v1, /device:TPU:2, one launch (start us, length us, event | category | flops | bytes accessed | tf_op | source)
XLA Modules:
  0.0 57.3 jit_solution(14861010599708375133)
XLA Ops:
  0.6 0.0 copy-start
  0.6 0.0 copy-start.1
  0.7 0.0 copy-start.2
  0.7 2.0 %halo.1 = (f32[56,768]{1,0:T(8,128)}, f32[56,768]{1,0:T(8,128)}, f32[1,128]{1,0:T(1,128)}) custom-call(s32[1]{0:T(128)} %bitcast.refs_0_.group, f32[12]{0:T(128)} %refs_1_.1, f32[3,12,2048]{2,1,0:T(8,128)} %fields.1, s32[12,1,2048]{2,1,0:T(1,128)} %index.3, f32[12,1,2048]{2,1,0:T(1,128)} %weight.3, s32[6,2048]{1,0:T(8,128)} %nbr.3, f32[6,2048]{1,0:T(8,128)} %lap.1, ...), custom_call_target="tpu_custom_call" | custom-call | tf_op jit(solution)/shard_map/halo/pallas_call | solution.py:319
  2.7 0.1 collective-permute-start
  2.8 0.0 copy-start.7
  2.8 6.4 %collective-permute-start.1 = (f32[56,768]{1,0:T(8,128)}, f32[56,768]{1,0:T(8,128)S(1)}, u32[]{:S(2)}, u32[]{:S(2)}) collective-permute-start(f32[56,768]{1,0:T(8,128)} %get-tuple-element.16), channel_id=1, source_target_pairs={{8,0},{16,8},{24,16},{32,24},{40,32},{48,40},{56,48},{64,56},{72,6... | collective-permute-start | bytes 516104 | tf_op jit(solution)/shard_map/ppermute | solution.py:333
  9.2 0.0 copy-done
  9.2 0.0 copy-done.1
  9.2 0.0 copy-done.2
  9.2 0.0 copy-done.7
  9.2 0.0 copy-start.3
  9.2 0.0 copy-start.4
  9.2 0.0 copy-start.5
  9.2 5.7 %inner.1 = (f32[40,2048]{1,0:T(8,128)S(1)}, f32[40,1024]{1,0:T(8,128)S(1)}) custom-call(f32[3,12,2048]{2,1,0:T(8,128)S(1)} %copy-done, s32[12,1,2048]{2,1,0:T(1,128)S(1)} %copy-done.1, f32[12,1,2048]{2,1,0:T(1,128)S(1)} %copy-done.2, f32[1,128]{1,0:T(1,128)S(1)} %copy-done.7), custom_call_target="tpu_custom_call" | custom-call | tf_op jit(solution)/shard_map/inner/pallas_call | solution.py:334
  15.0 0.0 collective-permute-done.left
  15.0 0.0 collective-permute-done.1.right
  15.0 0.0 copy-done.3
  15.0 0.0 copy-done.4
  15.0 0.0 copy-done.5
  15.0 12.6 %outer.1 = (f32[2,12,2048]{2,1,0:T(8,128)S(1)}, f32[8,16,768]{2,1,0:T(8,128)}) custom-call(f32[40,2048]{1,0:T(8,128)S(1)} %get-tuple-element.13.packed, f32[40,1024]{1,0:T(8,128)S(1)} %get-tuple-element.14.inner, f32[56,768]{1,0:T(8,128)S(1)} %collective-permute-done.left, f32[56,768]{1,0:T(8,128)S(1)} %collective-permute-done.1.right, ...), custom_call_target="tpu_custom_call" | custom-call | tf_op jit(solution)/shard_map/outer/pallas_call | solution.py:341
  27.6 0.0 copy-start.9
  27.6 7.3 %all-to-all-start = ((f32[8,16,768]{2,1,0:T(8,128)}), f32[8,16,768]{2,1,0:T(8,128)S(1)}, u32[]{:S(2)}, u32[]{:S(2)}) async-start(f32[8,16,768]{2,1,0:T(8,128)} %get-tuple-element.18), calls=%async_computation | async-start | bytes 786432 | tf_op jit(solution)/shard_map/all_to_all | solution.py:368
  34.9 0.0 copy-done.9
  34.9 0.1 copy.13
  35.0 0.0 copy-start.8
  35.0 0.1 copy.14.to_modes
  35.1 0.7 %copy-done.8 = f32[96,96]{1,0:T(8,128)S(1)} copy-done((f32[96,96]{1,0:T(8,128)S(1)}, f32[96,96]{1,0:T(8,128)}, u32[]{:S(2)}) %copy-start.8) | copy-done | bytes 36888
  35.8 0.0 copy-start.6
  35.8 0.8 %copy-done.6 = f32[6,2048]{1,0:T(8,128)S(1)} copy-done((f32[6,2048]{1,0:T(8,128)S(1)}, f32[6,2048]{1,0:T(8,128)}, u32[]{:S(2)}) %copy-start.6) | copy-done | bytes 49176
  36.6 1.1 %band.1 = (bf16[4,384,128]{2,1,0:T(8,128)(2,1)S(1)}, bf16[4,384,128]{2,1,0:T(8,128)(2,1)S(1)}, f32[1,768]{1,0:T(1,128)S(1)}) custom-call(s32[1]{0:T(128)} %bitcast.refs_0_.group, f32[56,768]{1,0:T(8,128)S(1)} %collective-permute-done.left, f32[56,768]{1,0:T(8,128)S(1)} %collective-permute-done.1.right, s32[6,2048]{1,0:T(8,128)S(1)} %copy-done.3, ...), custom_call_target="tpu_custom_call" | custom-call | tf_op jit(solution)/shard_map/band/pallas_call | solution.py:360
  37.7 5.5 %all-to-all-done.got = f32[8,16,768]{2,1,0:T(8,128)S(1)} async-done(((f32[8,16,768]{2,1,0:T(8,128)}), f32[8,16,768]{2,1,0:T(8,128)S(1)}, u32[]{:S(2)}, u32[]{:S(2)}) %all-to-all-start) | async-done | bytes 393248 | tf_op jit(solution)/shard_map/all_to_all | solution.py:368
  43.2 2.0 %solve.1 = f32[8,16,256]{2,1,0:T(8,128)} custom-call(f32[8,16,768]{2,1,0:T(8,128)S(1)} %all-to-all-done.got, bf16[4,384,128]{2,1,0:T(8,128)(2,1)S(1)} %get-tuple-element.19.high, bf16[4,384,128]{2,1,0:T(8,128)(2,1)S(1)} %get-tuple-element.20.low, f32[1,768]{1,0:T(1,128)S(1)} %get-tuple-element.21.total, f32[96,128]{1,0:T(8,128)S(1)} %copy.14.to_modes, ...), custom_call_target="tpu_custom_call" | custom-call | tf_op jit(solution)/shard_map/solve/pallas_call | solution.py:375
  45.2 4.4 %all-to-all-start.1 = ((f32[8,16,256]{2,1,0:T(8,128)}), f32[8,16,256]{2,1,0:T(8,128)S(1)}, u32[]{:S(2)}, u32[]{:S(2)}) async-start(f32[8,16,256]{2,1,0:T(8,128)} %solve.1), calls=%async_computation.1 | async-start | bytes 262144 | tf_op jit(solution)/shard_map/all_to_all | solution.py:378
  49.6 0.8 %copy.15 = f32[2,12,2048]{2,0,1:T(2,128)} copy(f32[2,12,2048]{2,1,0:T(8,128)S(1)} %get-tuple-element.24) | data formatting | bytes 393216
  50.5 6.1 %all-to-all-done.1.got = f32[8,16,256]{2,1,0:T(8,128)S(1)} async-done(((f32[8,16,256]{2,1,0:T(8,128)}), f32[8,16,256]{2,1,0:T(8,128)S(1)}, u32[]{:S(2)}, u32[]{:S(2)}) %all-to-all-start.1) | async-done | bytes 131104 | tf_op jit(solution)/shard_map/all_to_all | solution.py:378
  56.6 0.7 %place.1 = f32[12,2048]{1,0:T(8,128)} custom-call(f32[8,16,256]{2,1,0:T(8,128)S(1)} %all-to-all-done.1.got), custom_call_target="tpu_custom_call" | custom-call | tf_op jit(solution)/shard_map/place/pallas_call | solution.py:379
  (4 shorter events, 0.0 us)
Async XLA Ops:
  0.6 8.6 %copy-start = (f32[3,12,2048]{2,1,0:T(8,128)S(1)}, f32[3,12,2048]{2,1,0:T(8,128)}, u32[]{:S(2)}) copy-start(f32[3,12,2048]{2,1,0:T(8,128)} %fields.1) | copy-start | bytes 884740
  0.6 8.5 %copy-start.1 = (s32[12,1,2048]{2,1,0:T(1,128)S(1)}, s32[12,1,2048]{2,1,0:T(1,128)}, u32[]{:S(2)}) copy-start(s32[12,1,2048]{2,1,0:T(1,128)} %index.3) | copy-start | bytes 294916
  0.7 8.5 %copy-start.2 = (f32[12,1,2048]{2,1,0:T(1,128)S(1)}, f32[12,1,2048]{2,1,0:T(1,128)}, u32[]{:S(2)}) copy-start(f32[12,1,2048]{2,1,0:T(1,128)} %weight.3) | copy-start | bytes 294916
  2.7 12.3 %collective-permute-start = (f32[56,768]{1,0:T(8,128)}, f32[56,768]{1,0:T(8,128)S(1)}, u32[]{:S(2)}, u32[]{:S(2)}) collective-permute-start(f32[56,768]{1,0:T(8,128)} %get-tuple-element.15), channel_id=1, source_target_pairs={{0,8},{8,16},{16,24},{24,32},{32,40},{40,48},{48,56},{56,64},{64,7... | collective-permute-start | bytes 516104 | tf_op jit(solution)/shard_map/ppermute | solution.py:332
  2.8 6.4 %copy-start.7 = (f32[1,128]{1,0:T(1,128)S(1)}, f32[1,128]{1,0:T(1,128)}, u32[]{:S(2)}) copy-start(f32[1,128]{1,0:T(1,128)} %get-tuple-element.12.coef_row) | copy-start | bytes 1540
  2.8 12.2 %collective-permute-start.1 = (f32[56,768]{1,0:T(8,128)}, f32[56,768]{1,0:T(8,128)S(1)}, u32[]{:S(2)}, u32[]{:S(2)}) collective-permute-start(f32[56,768]{1,0:T(8,128)} %get-tuple-element.16), channel_id=1, source_target_pairs={{8,0},{16,8},{24,16},{32,24},{40,32},{48,40},{56,48},{64,56},{72,6... | collective-permute-start | bytes 516104 | tf_op jit(solution)/shard_map/ppermute | solution.py:333
  9.2 5.8 %copy-start.3 = (s32[6,2048]{1,0:T(8,128)S(1)}, s32[6,2048]{1,0:T(8,128)}, u32[]{:S(2)}) copy-start(s32[6,2048]{1,0:T(8,128)} %nbr.3) | copy-start | bytes 147460
  9.2 5.8 %copy-start.4 = (f32[6,2048]{1,0:T(8,128)S(1)}, f32[6,2048]{1,0:T(8,128)}, u32[]{:S(2)}) copy-start(f32[6,2048]{1,0:T(8,128)} %ex.1) | copy-start | bytes 147460
  9.2 5.8 %copy-start.5 = (f32[6,2048]{1,0:T(8,128)S(1)}, f32[6,2048]{1,0:T(8,128)}, u32[]{:S(2)}) copy-start(f32[6,2048]{1,0:T(8,128)} %ey.1) | copy-start | bytes 147460
  27.6 7.3 %copy-start.9 = (f32[96,96]{1,0:T(8,128)S(1)}, f32[96,96]{1,0:T(8,128)}, u32[]{:S(2)}) copy-start(f32[96,96]{1,0:T(8,128)} %param.17) | copy-start | bytes 110596
  27.6 15.6 %all-to-all-start = ((f32[8,16,768]{2,1,0:T(8,128)}), f32[8,16,768]{2,1,0:T(8,128)S(1)}, u32[]{:S(2)}, u32[]{:S(2)}) async-start(f32[8,16,768]{2,1,0:T(8,128)} %get-tuple-element.18), calls=%async_computation | async-start | bytes 786432 | tf_op jit(solution)/shard_map/all_to_all | solution.py:368
  35.0 0.8 %copy-start.8 = (f32[96,96]{1,0:T(8,128)S(1)}, f32[96,96]{1,0:T(8,128)}, u32[]{:S(2)}) copy-start(f32[96,96]{1,0:T(8,128)} %param.18) | copy-start | bytes 110596
  35.8 0.8 %copy-start.6 = (f32[6,2048]{1,0:T(8,128)S(1)}, f32[6,2048]{1,0:T(8,128)}, u32[]{:S(2)}) copy-start(f32[6,2048]{1,0:T(8,128)} %lap.1) | copy-start | bytes 147460
  45.2 11.4 %all-to-all-start.1 = ((f32[8,16,256]{2,1,0:T(8,128)}), f32[8,16,256]{2,1,0:T(8,128)S(1)}, u32[]{:S(2)}, u32[]{:S(2)}) async-start(f32[8,16,256]{2,1,0:T(8,128)} %solve.1), calls=%async_computation.1 | async-start | bytes 262144 | tf_op jit(solution)/shard_map/all_to_all | solution.py:378

commit v2 on v1

--- a/solution.py
+++ b/solution.py
@@ -16,7 +16,6 @@
 SIDES = 6
 GROUPS = 8
 ROWS = 12
-SLAB = 16
 LANES = 128
 EDGE = 256
 FIELD_EDGE = EDGE + REACH
@@ -27,6 +26,8 @@
 TILES = 9
 INNER_LO = FIELD_EDGE // LANES
 INNER = (CELLS - 2 * REACH) // LANES
+MATRIX = 8
+HALF = WINDOW // 2
 HALO_ROWS = 56
 COUPLING = 0.5
 
@@ -80,52 +81,140 @@
     coef_row[...] = row
 
 
-def stencil_block(x, col, away, weight, away_col):
+def split(v):
+    high = v.astype(bf16)
+    return high, (v - high.astype(f32)).astype(bf16)
+
+
+def split_tiles(dst, first, src, src_col, count):
+    for t in range(count):
+        high, low = split(src[0:40, src_col + t * LANES : src_col + (t + 1) * LANES])
+        dst[first + t, :, 0:LANES] = high
+        dst[first + t, :, LANES:] = low
+
+
+def stencil_block(x, slabs, first, col, away, weight, away_col):
     groups = 5
     acc = [jnp.zeros((8, LANES), f32) for _ in range(groups)]
     lane = lax.broadcasted_iota(jnp.int32, (1, LANES), 1)
-    for p in range(POINTS):
+    slot = lax.broadcasted_iota(jnp.int32, (LANES, LANES), 0).astype(bf16)
+    ones = jnp.ones((LANES, LANES), bf16)
+    near = slabs[pl.ds(first, TILES)].reshape(TILES * 8 * groups, 2 * LANES)
+
+    def locate(p):
         at = away[p, :, pl.ds(away_col, LANES)] + (lane + REACH)
-        at = jnp.broadcast_to(at, (8, LANES))
         w = jnp.broadcast_to(weight[p, :, pl.ds(away_col, LANES)], (8, LANES))
-        inside = at & (LANES - 1)
-        tile = at >> 7
+        return at & (LANES - 1), jnp.broadcast_to(at >> 7, (8, LANES)), w
+
+    def add(part, tile, w):
         picked = [None] * groups
         for t in range(TILES):
             mask = tile == t
             for g in range(groups):
-                part = x[8 * g : 8 * g + 8, pl.ds(col + t * LANES, LANES)]
-                part = jnp.take_along_axis(part, inside, axis=1, mode="promise_in_bounds")
-                picked[g] = part if t == 0 else jnp.where(mask, part, picked[g])
+                picked[g] = part(t, g) if t == 0 else jnp.where(mask, part(t, g), picked[g])
         for g in range(groups):
             acc[g] = acc[g] + w * picked[g]
+
+    def one_hot(inside):
+        at = jnp.broadcast_to(inside.astype(f32), (LANES, LANES)).astype(bf16)
+        return jnp.where(slot == at, ones, jnp.zeros_like(ones))
+
+    def gathered(p):
+        inside, tile, w = locate(p)
+        inside = jnp.broadcast_to(inside, (8, LANES))
+
+        def part(t, g):
+            rows = x[8 * g : 8 * g + 8, pl.ds(col + t * LANES, LANES)]
+            return jnp.take_along_axis(rows, inside, axis=1, mode="promise_in_bounds")
+
+        add(part, tile, w)
+
+    plain = list(range(MATRIX, POINTS))
+    for pair in range(0, MATRIX, 2):
+        points = [locate(p) for p in (pair, pair + 1)]
+        hot = jnp.concatenate([one_hot(inside) for inside, _, _ in points], axis=1)
+        rows = jnp.dot(near, jnp.concatenate([hot, hot], axis=0), preferred_element_type=f32)
+        if plain:
+            gathered(plain.pop(0))
+        for i, (_, tile, w) in enumerate(points):
+            c = slice(i * LANES, (i + 1) * LANES)
+            add(lambda t, g: rows[40 * t + 8 * g : 40 * t + 8 * g + 8, c], tile, w)
+    for p in plain:
+        gathered(p)
     return acc
 
 
-def inner_kernel(fields, index, weight, coef_row, packed, upstream, away):
+def right_side_block(up, up_col, side, side_x, side_y, col):
+    lane = lax.broadcasted_iota(jnp.int32, (1, LANES), 1)
+    upper = lax.broadcasted_iota(jnp.int32, (8, LANES), 0) < 4
+    rows = (0, 8, 24)
+    here = [up[r : r + 8, pl.ds(up_col + LANES, LANES)] for r in rows]
+    acc = [jnp.zeros((8, LANES), f32) for _ in rows]
+    for k in range(SIDES):
+        at = jnp.broadcast_to(side[k : k + 1, pl.ds(col, LANES)] + (lane + LANES), (8, LANES))
+        inside = at & (LANES - 1)
+        tile = at >> 7
+        wx = jnp.broadcast_to(side_x[k : k + 1, pl.ds(col, LANES)], (8, LANES))
+        wy = jnp.broadcast_to(side_y[k : k + 1, pl.ds(col, LANES)], (8, LANES))
+        weights = (wx, wy, jnp.where(upper, wx, wy))
+        for g, r in enumerate(rows):
+            picked = None
+            for t in range(3):
+                part = up[r : r + 8, pl.ds(up_col + t * LANES, LANES)]
+                part = jnp.take_along_axis(part, inside, axis=1, mode="promise_in_bounds")
+                picked = part if t == 0 else jnp.where(tile == t, part, picked)
+            acc[g] = acc[g] + weights[g] * (picked - here[g])
+    top = up[16:24, pl.ds(up_col + LANES, LANES)] - COUPLING * (acc[0] + acc[1])
+    rest = up[32:36, pl.ds(up_col + LANES, LANES)] - COUPLING * (acc[2][0:4] + acc[2][4:8])
+    return top, rest
+
+
+def inner_kernel(
+    fields, index, weight, nbr, ex, ey, coef_row,
+    packed, slabs, upstream, right, away, side,
+):
     pack_fields(packed, 0, fields, 0, CELLS)
     packed[36:37, 0:LANES] = coef_row[...]
+    split_tiles(slabs, 0, packed, 0, CELLS // LANES)
     own = lax.broadcasted_iota(jnp.int32, (1, CELLS), 1)
     for p in range(POINTS):
         away[p] = index[p] - REACH - own
-
-    def body(b, carry):
+    side[...] = nbr[...] - NBR_REACH - own
+
+    def stencil(b, carry):
         col = pl.multiple_of(b * LANES, LANES)
-        acc = stencil_block(packed, col, away, weight, pl.multiple_of(col + REACH, LANES))
+        acc = stencil_block(
+            packed, slabs, b, col, away, weight, pl.multiple_of(col + REACH, LANES)
+        )
         for g in range(5):
             upstream[8 * g : 8 * g + 8, pl.ds(col, LANES)] = acc[g]
         return carry
 
-    lax.fori_loop(0, INNER, body, 0)
+    lax.fori_loop(0, INNER, stencil, 0, unroll=4)
+
+    def finish(b, carry):
+        col = pl.multiple_of(b * LANES, LANES)
+        top, rest = right_side_block(
+            upstream, col, side, ex, ey, pl.multiple_of(col + REACH + LANES, LANES)
+        )
+        right[0:8, pl.ds(col, LANES)] = top
+        right[8:12, pl.ds(col, LANES)] = rest
+        return carry
+
+    lax.fori_loop(0, INNER - 2, finish, 0, unroll=2)
 
 
 def outer_kernel(
-    packed, inner, left, right, index, weight, nbr, ex, ey,
-    winds, send, x, up, away, w_all, side, side_x, side_y, rs,
+    packed, own_slabs, inner, inner_right, left, right, index, weight, nbr, ex, ey,
+    winds, send, x, slabs, up, away, w_all, side, side_x, side_y, rs, rest_rs,
 ):
+    halo_tiles = FIELD_EDGE // LANES
     x[:, 0:FIELD_EDGE] = left[0:40, :]
     x[:, FIELD_EDGE : FIELD_EDGE + CELLS] = packed[...]
     x[:, FIELD_EDGE + CELLS :] = right[0:40, :]
+    split_tiles(slabs, 0, left, 0, halo_tiles)
+    slabs[halo_tiles : halo_tiles + CELLS // LANES] = own_slabs[...]
+    split_tiles(slabs, halo_tiles + CELLS // LANES, right, 0, halo_tiles)
     own = lax.broadcasted_iota(jnp.int32, (1, CELLS), 1)
     mid = slice(EDGE, EDGE + CELLS)
     for halo, cells in ((left, slice(0, EDGE)), (right, slice(EDGE + CELLS, WIDE))):
@@ -136,9 +225,12 @@
         side[4:6, cells] = halo[52:54, 2 * EDGE :].astype(jnp.int32)
         side_x[:, cells] = halo[40:46, 2 * EDGE :]
         side_y[:, cells] = halo[46:52, 2 * EDGE :]
-    for p in range(POINTS):
-        away[p, :, mid] = index[p] - REACH - own
-        w_all[p, :, mid] = weight[p]
+    for start in (0, CELLS - REACH):
+        there = start + lax.broadcasted_iota(jnp.int32, (1, REACH), 1)
+        cells = slice(EDGE + start, EDGE + start + REACH)
+        for p in range(POINTS):
+            away[p, :, cells] = index[p, :, start : start + REACH] - REACH - there
+            w_all[p, :, cells] = weight[p, :, start : start + REACH]
     side[:, mid] = nbr[...] - NBR_REACH - own
     side_x[:, mid] = ex[...]
     side_y[:, mid] = ey[...]
@@ -149,59 +241,48 @@
     up[:, first : first + INNER * LANES] = inner[...]
 
     def stencil(i, carry):
-        b = jnp.where(i < INNER_LO, i, i + INNER)
-        col = pl.multiple_of(b * LANES, LANES)
-        acc = stencil_block(x, col, away, w_all, col)
-        for g in range(5):
-            up[8 * g : 8 * g + 8, pl.ds(col + LANES, LANES)] = acc[g]
+        for b in (i, i + INNER_LO + INNER):
+            col = pl.multiple_of(b * LANES, LANES)
+            acc = stencil_block(x, slabs, b, col, away, w_all, col)
+            for g in range(5):
+                up[8 * g : 8 * g + 8, pl.ds(col + LANES, LANES)] = acc[g]
         return carry
 
-    lax.fori_loop(0, WIDE_BLOCKS - INNER, stencil, 0)
+    lax.fori_loop(0, INNER_LO, stencil, 0, unroll=3)
 
     for field in range(2):
         cells = slice(LANES + EDGE, LANES + EDGE + CELLS)
         winds[field, 0:8, :] = up[8 * field : 8 * field + 8, cells]
         winds[field, 8:12, :] = up[24 + 4 * field : 28 + 4 * field, cells]
 
+    first = (INNER_LO + 1) * LANES
+    last = first + (INNER - 2) * LANES
+    rs[:, first:last] = inner_right[0:8, :]
+    rest_rs[0:4, HALF + first : HALF + last] = inner_right[8:12, :]
+    rest_rs[4:8, first:last] = inner_right[8:12, :]
+
+    def finish(i, carry):
+        for b in (i, i + INNER_LO + INNER - 1):
+            col = pl.multiple_of(b * LANES, LANES)
+            top, rest = right_side_block(up, col, side, side_x, side_y, col)
+            rs[:, pl.ds(col, LANES)] = top
+            rest_rs[0:4, pl.ds(col + HALF, LANES)] = rest
+            rest_rs[4:8, pl.ds(col, LANES)] = rest
+        return carry
+
+    lax.fori_loop(0, INNER_LO + 1, finish, 0)
+
     lane = lax.broadcasted_iota(jnp.int32, (1, LANES), 1)
-    upper = lax.broadcasted_iota(jnp.int32, (8, LANES), 0) < 4
-
-    def divergence(b, carry):
-        col = pl.multiple_of(b * LANES, LANES)
-        rows = (0, 8, 24)
-        here = [up[r : r + 8, pl.ds(col + LANES, LANES)] for r in rows]
-        acc = [jnp.zeros((8, LANES), f32) for _ in rows]
-        for k in range(SIDES):
-            at = jnp.broadcast_to(side[k : k + 1, pl.ds(col, LANES)] + (lane + LANES), (8, LANES))
-            inside = at & (LANES - 1)
-            tile = at >> 7
-            wx = jnp.broadcast_to(side_x[k : k + 1, pl.ds(col, LANES)], (8, LANES))
-            wy = jnp.broadcast_to(side_y[k : k + 1, pl.ds(col, LANES)], (8, LANES))
-            weights = (wx, wy, jnp.where(upper, wx, wy))
-            for g, r in enumerate(rows):
-                picked = None
-                for t in range(3):
-                    part = up[r : r + 8, pl.ds(col + t * LANES, LANES)]
-                    part = jnp.take_along_axis(part, inside, axis=1, mode="promise_in_bounds")
-                    picked = part if t == 0 else jnp.where(tile == t, part, picked)
-                acc[g] = acc[g] + weights[g] * (picked - here[g])
-        h0 = up[16:24, pl.ds(col + LANES, LANES)]
-        h1 = up[32:36, pl.ds(col + LANES, LANES)]
-        rs[0:8, pl.ds(col, LANES)] = h0 - COUPLING * (acc[0] + acc[1])
-        rs[8:12, pl.ds(col, LANES)] = h1 - COUPLING * (acc[2][0:4] + acc[2][4:8])
-        return carry
-
-    lax.fori_loop(0, WIDE_BLOCKS, divergence, 0)
-
-    rs[12:16, :] = jnp.zeros((4, WIDE), f32)
+    coef = packed[36:37, 0:LANES]
     for j in range(GROUPS):
-        send[j] = rs[:, j * CHUNK : j * CHUNK + WINDOW]
-        send[j, 12:13, 0:LANES] = packed[36:37, 0:LANES]
-
-
-def split(v):
-    high = v.astype(bf16)
-    return high, (v - high.astype(f32)).astype(bf16)
+        col = j * CHUNK
+        send[j, :, 0:WINDOW] = rs[:, col : col + WINDOW]
+        send[j, :, WINDOW:] = rest_rs[:, HALF + col : 2 * HALF + col]
+        send[j, 0:1, 0:LANES] = jnp.where(lane < NBR_REACH, coef, rs[0:1, col : col + LANES])
+        col = col + WINDOW - LANES
+        send[j, 0:1, WINDOW - LANES : WINDOW] = jnp.where(
+            lane < NBR_REACH, rs[0:1, col : col + LANES], coef
+        )
 
 
 def dot3(a, b):
@@ -234,17 +315,24 @@
         high[b], low[b] = split(matrix)
 
 
-def solve_kernel(got, high, low, total, to_modes, from_modes, out):
-    levels = got[...].reshape(GROUPS * SLAB, WINDOW)
+def solve_kernel(got, high, low, total, to_first, to_second, from_first, from_second, out):
     modes = GROUPS * ROWS
-    coef_row = got[0, 12:13, 0:LANES]
-    for j in range(1, GROUPS):
-        coef_row = coef_row + got[j, 12:13, 0:LANES]
+    lane = lax.broadcasted_iota(jnp.int32, (1, LANES), 1)
+    left = got[:, 0, 0:LANES]
+    right = got[:, 0, WINDOW - LANES : WINDOW]
+    coef_row = jnp.sum(jnp.where(lane < NBR_REACH, left, right), axis=0, keepdims=True)
     eye = lax.broadcasted_iota(jnp.int32, (modes, LANES), 0) == lax.broadcasted_iota(
         jnp.int32, (modes, LANES), 1
     )
     coef = jnp.sum(jnp.where(eye, coef_row, 0.0), axis=1, keepdims=True)
-    rhs = dot3(split(to_modes[...]), split(levels))
+    rows = GROUPS * 8
+    main = split(got[:, :, 0:WINDOW].reshape(rows, WINDOW))
+    rest = split(got[:, :, WINDOW:].reshape(rows, HALF))
+    halves = []
+    for matrix, cols in ((to_first, slice(0, HALF)), (to_second, slice(HALF, WINDOW))):
+        levels = tuple(jnp.concatenate([m[:, cols], r], axis=0) for m, r in zip(main, rest))
+        halves.append(dot3(split(matrix[...]), levels))
+    rhs = jnp.concatenate(halves, axis=1)
     inverse = 1.0 / (1.0 + coef * total[...])
     rhs = rhs * inverse
     scaled = coef * inverse
@@ -256,24 +344,44 @@
     cols = [slice(b * LANES, (b + 1) * LANES) for b in range(6)]
     iterate = [steps[0] * rhs[:, c] for c in cols]
     for sweep, blocks in ((1, (1, 2, 3, 4)), (2, (1, 2, 3, 4)), (3, (2, 3))):
-        parts = [split(v) for v in iterate]
+        parts = [jnp.concatenate(split(v), axis=0) for v in iterate]
         step = steps[sweep]
         fresh = list(iterate)
         for b in blocks:
-            near = [jnp.concatenate([parts[b + o][i] for o in (-1, 0, 1)], axis=1) for i in (0, 1)]
-            moved = dot3(near, (high[b - 1], low[b - 1]))
+            near = jnp.concatenate(parts[b - 1 : b + 2], axis=1)
+            both = jnp.concatenate([high[b - 1], low[b - 1]], axis=1)
+            four = jnp.dot(near, both, preferred_element_type=f32)
+            moved = four[:modes, :LANES] + (
+                four[modes:, :LANES] + four[:modes, LANES:] + four[modes:, LANES:]
+            )
             fresh[b] = (1.0 - step) * iterate[b] + step * (
                 rhs[:, cols[b]] + scaled[:, cols[b]] * moved
             )
         iterate = fresh
-    solved = jnp.concatenate([iterate[2], iterate[3]], axis=1)
-    height = dot3(split(from_modes[...]), split(solved))
-    out[...] = height.reshape(GROUPS, SLAB, CHUNK)
+    first = dot3(split(from_first[...]), split(iterate[2]))
+    second = dot3(split(from_second[...]), split(iterate[3]))
+    shape = (GROUPS, 8, LANES)
+    out[:, :, 0:LANES] = first[:rows].reshape(shape)
+    out[:, :, LANES:CHUNK] = second[:rows].reshape(shape)
+    out[:, :, CHUNK:] = (first[rows:] + second[rows:]).reshape(shape)
 
 
 def place_kernel(got, out):
     for j in range(GROUPS):
-        out[:, j * CHUNK : (j + 1) * CHUNK] = got[j, 0:ROWS, :]
+        col = j * CHUNK
+        out[0:8, col : col + CHUNK] = got[j, :, 0:CHUNK]
+        out[8:12, col : col + LANES] = got[j, 0:4, CHUNK:]
+        out[8:12, col + LANES : col + CHUNK] = got[j, 4:8, CHUNK:]
+
+
+def slab_order(matrix):
+    groups = matrix.reshape(GROUPS, ROWS, -1)
+    main = groups[:, 0:8].reshape(GROUPS * 8, -1)
+    pads = (((0, 0), (0, 4), (0, 0)), ((0, 0), (4, 0), (0, 0)))
+    return [
+        jnp.concatenate([main, jnp.pad(groups[:, 8:12], pad).reshape(GROUPS * 8, -1)], axis=0)
+        for pad in pads
+    ]
 
 
 def call(kernel, outs, scratch=(), name=None, smem=0, n_in=0, space=pltpu.VMEM, vmem=32):
@@ -331,30 +439,38 @@
     )
     left = lax.ppermute(tail, "patch", [(i, (i + 1) % patches) for i in range(patches)])
     right = lax.ppermute(head, "patch", [((i + 1) % patches, i) for i in range(patches)])
-    packed, inner = call(
+    tiles = CELLS // LANES
+    packed, slabs, inner, inner_right = call(
         inner_kernel,
-        [((40, CELLS), f32), ((40, INNER * LANES), f32)],
-        [pltpu.VMEM((POINTS, 1, CELLS), jnp.int32)],
+        [
+            ((40, CELLS), f32),
+            ((tiles, 40, 2 * LANES), bf16),
+            ((40, INNER * LANES), f32),
+            ((ROWS, (INNER - 2) * LANES), f32),
+        ],
+        [pltpu.VMEM((POINTS, 1, CELLS), jnp.int32), pltpu.VMEM((SIDES, CELLS), jnp.int32)],
         name="inner",
-        n_in=4,
-    )(fields, stencil_index, stencil_weight, coef_row)
+        n_in=7,
+    )(fields, stencil_index, stencil_weight, neighbours, edge_x, edge_y, coef_row)
     new_winds, send = call(
         outer_kernel,
-        [((2, ROWS, CELLS), f32), ((GROUPS, SLAB, WINDOW), f32)],
+        [((2, ROWS, CELLS), f32), ((GROUPS, 8, WINDOW + HALF), f32)],
         [
             pltpu.VMEM((40, CELLS + 2 * FIELD_EDGE), f32),
+            pltpu.VMEM((tiles + 2 * FIELD_EDGE // LANES, 40, 2 * LANES), bf16),
             pltpu.VMEM((40, WIDE + 2 * LANES), f32),
             pltpu.VMEM((POINTS, 1, WIDE), jnp.int32),
             pltpu.VMEM((POINTS, 1, WIDE), f32),
             pltpu.VMEM((SIDES, WIDE), jnp.int32),
             pltpu.VMEM((SIDES, WIDE), f32),
             pltpu.VMEM((SIDES, WIDE), f32),
-            pltpu.VMEM((SLAB, WIDE), f32),
+            pltpu.VMEM((8, WIDE), f32),
+            pltpu.VMEM((8, WIDE + HALF), f32),
         ],
         name="outer",
-        n_in=9,
+        n_in=11,
     )(
-        packed, inner, left, right, stencil_index, stencil_weight,
+        packed, slabs, inner, inner_right, left, right, stencil_index, stencil_weight,
         neighbours, edge_x, edge_y,
     )
     high, low, total = call(
@@ -366,14 +482,9 @@
         n_in=5,
     )(group[None], left, right, neighbours, lap_weight)
     got = lax.all_to_all(send, "lev", split_axis=0, concat_axis=0, tiled=True)
-    pad = ((0, 0), (0, 0), (0, SLAB - ROWS))
-    modes = GROUPS * ROWS
-    to_wide = jnp.pad(to_modes.reshape(modes, GROUPS, ROWS), pad).reshape(modes, GROUPS * SLAB)
-    from_wide = jnp.pad(
-        from_modes.reshape(GROUPS, ROWS, modes), ((0, 0), (0, SLAB - ROWS), (0, 0))
-    ).reshape(GROUPS * SLAB, modes)
-    heights = call(solve_kernel, [((GROUPS, SLAB, CHUNK), f32)], name="solve", n_in=6)(
-        got, high, low, total, to_wide, from_wide
+    to_slabs = [m.T for m in slab_order(to_modes.T)]
+    heights = call(solve_kernel, [((GROUPS, 8, CHUNK + LANES), f32)], name="solve", n_in=8)(
+        got, high, low, total, *to_slabs, *slab_order(from_modes)
     )
     heights = lax.all_to_all(heights, "lev", split_axis=0, concat_axis=0, tiled=True)
     new_height = call(place_kernel, [((ROWS, CELLS), f32)], name="place", n_in=1)(heights)

time: 57.7 us -> 47.6 us (0.82)
  Pallas kernels: 24 us -> 13.9 us
    pallas_call x3, Pallas kernels: 20.3 us -> 10.2 us  [the longest x1 5.54 us: per_device(): call(outer_kernel, [((2, ROWS, CELLS), f32), ((GROUPS, 8, WINDOW + HALF),...]
    unnamed x22 -> x21, local copies, waits for them, and re-layouts: 2.47 us -> 2.45 us
  transfers between devices with their start and end apart: 4 -> 4, of which waited for: 2 -> 2; matrix products, arithmetic and copies ran while one was open for 2% -> 3% of each run, Pallas kernels for 12% -> 8%
where the time goes in v2:
time: 47.6 us; the launch traced here: 47.2 us
  starting transfers between devices  18.1 us (38%)
  Pallas kernels  13.9 us (29%)
  waiting for transfers between devices  11.5 us (24%)
  local copies, waits for them, and re-layouts  2.83 us (6%)
  between operations  0.88 us (2%)
    all_to_all x1, starting transfers between devices, per_device(): got = lax.all_to_all(send, 'lev', split_axis=0, concat_axis=0, tiled=True)  7.17 us
    ppermute x1, starting transfers between devices, per_device(): lax.ppermute(head, 'patch', [((i + 1) % patches, i) for i in range(patche...  6.38 us
    all_to_all x1, waiting for transfers between devices, per_device(): lax.all_to_all(heights, 'lev', split_axis=0, concat_axis=0, tiled=True)  5.95 us
    pallas_call x1, Pallas kernels, per_device(): call(outer_kernel, [((2, ROWS, CELLS), f32), ((GROUPS, 8, WINDOW + HALF),...  5.54 us
    all_to_all x1, waiting for transfers between devices, per_device(): got = lax.all_to_all(send, 'lev', split_axis=0, concat_axis=0, tiled=True)  5.51 us
    all_to_all x1, starting transfers between devices, per_device(): lax.all_to_all(heights, 'lev', split_axis=0, concat_axis=0, tiled=True)  4.44 us
    pallas_call x1, Pallas kernels, per_device(): call(inner_kernel, [((40, CELLS), f32), ((tiles, 40, 2 * LANES), bf16), (...  2.86 us
    unnamed x21, local copies, waits for them, and re-layouts  2.45 us
  transfers between devices with their start and end apart: 4, of which 2 were waited for; matrix products, arithmetic and copies ran while one was open for 3% of the time, Pallas kernels for 8%

profile of v2, /device:TPU:2, one launch (start us, length us, event | category | flops | bytes accessed | tf_op | source)
XLA Modules:
  0.0 47.2 jit_solution(13608590245899870978)
XLA Ops:
  0.6 0.0 copy-start
  0.6 0.0 copy-start.1
  0.7 0.0 copy-start.2
  0.7 0.0 copy-start.3
  0.7 0.0 copy-start.4
  0.7 0.0 copy-start.5
  0.7 2.0 %halo.1 = (f32[56,768]{1,0:T(8,128)}, f32[56,768]{1,0:T(8,128)}, f32[1,128]{1,0:T(1,128)}) custom-call(s32[1]{0:T(128)} %bitcast.refs_0_.group, f32[12]{0:T(128)} %refs_1_.1, f32[3,12,2048]{2,1,0:T(8,128)} %fields.1, s32[12,1,2048]{2,1,0:T(1,128)} %index.3, f32[12,1,2048]{2,1,0:T(1,128)} %weight.3, s32[6,2048]{1,0:T(8,128)} %nbr.5, f32[6,2048]{1,0:T(8,128)} %lap.1, ...), custom_call_target="tpu_custom_call" | custom-call | tf_op jit(solution)/shard_map/halo/pallas_call | solution.py:427
  2.7 0.1 collective-permute-start
  2.8 0.0 copy-start.7
  2.8 6.4 %collective-permute-start.1 = (f32[56,768]{1,0:T(8,128)}, f32[56,768]{1,0:T(8,128)S(1)}, u32[]{:S(2)}, u32[]{:S(2)}) collective-permute-start(f32[56,768]{1,0:T(8,128)} %get-tuple-element.20), channel_id=1, source_target_pairs={{8,0},{16,8},{24,16},{32,24},{40,32},{48,40},{56,48},{64,56},{72,6... | collective-permute-start | bytes 516104 | tf_op jit(solution)/shard_map/ppermute | solution.py:441
  9.2 0.0 copy-done
  9.2 0.0 copy-done.1
  9.2 0.0 copy-done.2
  9.2 0.0 copy-done.3
  9.2 0.0 copy-done.4
  9.2 0.0 copy-done.5
  9.2 0.0 copy-done.7
  9.2 0.0 copy-start.9
  9.2 2.9 %inner.1 = (f32[40,2048]{1,0:T(8,128)S(1)}, bf16[16,40,256]{2,1,0:T(8,128)(2,1)S(1)}, f32[40,1024]{1,0:T(8,128)S(1)}, f32[12,768]{1,0:T(8,128)S(1)}) custom-call(f32[3,12,2048]{2,1,0:T(8,128)S(1)} %copy-done, s32[12,1,2048]{2,1,0:T(1,128)S(1)} %copy-done.2, f32[12,1,2048]{2,1,0:T(1,128)S(1)} %copy-done.3, s32[6,2048]{1,0:T(8,128)S(1)} %copy-done.1, ...), custom_call_target="tpu_custom_call" | custom-call | tf_op jit(solution)/shard_map/inner/pallas_call | solution.py:443
  12.1 0.0 copy-done.9
  12.1 0.1 copy.13
  12.2 0.0 copy-start.8
  12.2 0.8 %copy-done.8 = f32[96,96]{1,0:T(8,128)S(1)} copy-done((f32[96,96]{1,0:T(8,128)S(1)}, f32[96,96]{1,0:T(8,128)}, u32[]{:S(2)}) %copy-start.8) | copy-done | bytes 36888
  13.1 0.0 collective-permute-done.left
  13.1 0.0 collective-permute-done.1.right
  13.1 5.5 %outer.1 = (f32[2,12,2048]{2,1,0:T(8,128)S(1)}, f32[8,8,1152]{2,1,0:T(8,128)}) custom-call(f32[40,2048]{1,0:T(8,128)S(1)} %get-tuple-element.15.packed, bf16[16,40,256]{2,1,0:T(8,128)(2,1)S(1)} %get-tuple-element.16.own_slabs, f32[40,1024]{1,0:T(8,128)S(1)} %get-tuple-element.17.inner, f32[12,768]{1,0:T(8,128)S(1)} %get-tuple-element.18.inner_right, ...), custom_call_target="tpu_custom_call" | custom-call | tf_op jit(solution)/shard_map/outer/pallas_call | solution.py:455
  18.6 7.2 %all-to-all-start = ((f32[8,8,1152]{2,1,0:T(8,128)}), f32[8,8,1152]{2,1,0:T(8,128)S(1)}, u32[]{:S(2)}, u32[]{:S(2)}) async-start(f32[8,8,1152]{2,1,0:T(8,128)} %get-tuple-element.22), calls=%async_computation | async-start | bytes 589824 | tf_op jit(solution)/shard_map/all_to_all | solution.py:484
  25.8 0.1 copy.17
  25.9 0.1 copy.14
  26.0 0.1 copy.15
  26.1 0.1 maximum_bitcast_fusion.1
  26.2 0.0 copy-start.6
  26.2 0.8 %copy-done.6 = f32[6,2048]{1,0:T(8,128)S(1)} copy-done((f32[6,2048]{1,0:T(8,128)S(1)}, f32[6,2048]{1,0:T(8,128)}, u32[]{:S(2)}) %copy-start.6) | copy-done | bytes 49176
  27.0 1.1 %band.1 = (bf16[4,384,128]{2,1,0:T(8,128)(2,1)S(1)}, bf16[4,384,128]{2,1,0:T(8,128)(2,1)S(1)}, f32[1,768]{1,0:T(1,128)S(1)}) custom-call(s32[1]{0:T(128)} %bitcast.refs_0_.group, f32[56,768]{1,0:T(8,128)S(1)} %collective-permute-done.left, f32[56,768]{1,0:T(8,128)S(1)} %collective-permute-done.1.right, s32[6,2048]{1,0:T(8,128)S(1)} %copy-done.1, ...), custom_call_target="tpu_custom_call" | custom-call | tf_op jit(solution)/shard_map/band/pallas_call | solution.py:476
  28.1 5.5 %all-to-all-done.got = f32[8,8,1152]{2,1,0:T(8,128)S(1)} async-done(((f32[8,8,1152]{2,1,0:T(8,128)}), f32[8,8,1152]{2,1,0:T(8,128)S(1)}, u32[]{:S(2)}, u32[]{:S(2)}) %all-to-all-start) | async-done | bytes 294944 | tf_op jit(solution)/shard_map/all_to_all | solution.py:484
  33.6 1.8 %solve.1 = f32[8,8,384]{2,1,0:T(8,128)} custom-call(f32[8,8,1152]{2,1,0:T(8,128)S(1)} %all-to-all-done.got, bf16[4,384,128]{2,1,0:T(8,128)(2,1)S(1)} %get-tuple-element.23.high, bf16[4,384,128]{2,1,0:T(8,128)(2,1)S(1)} %get-tuple-element.24.low, f32[1,768]{1,0:T(1,128)S(1)} %get-tuple-element.25.total, f32[96,128]{1,0:T(8,128)S(1)} %get-tuple-element.31.to_first, ...), custom_call_target="tpu_custom_call" | custom-call | tf_op jit(solution)/shard_map/solve/pallas_call | solution.py:486
  35.3 4.4 %all-to-all-start.1 = ((f32[8,8,384]{2,1,0:T(8,128)}), f32[8,8,384]{2,1,0:T(8,128)S(1)}, u32[]{:S(2)}, u32[]{:S(2)}) async-start(f32[8,8,384]{2,1,0:T(8,128)} %solve.1), calls=%async_computation.1 | async-start | bytes 196608 | tf_op jit(solution)/shard_map/all_to_all | solution.py:489
  39.8 0.8 %copy.18 = f32[2,12,2048]{2,0,1:T(2,128)} copy(f32[2,12,2048]{2,1,0:T(8,128)S(1)} %get-tuple-element.28) | data formatting | bytes 393216
  40.6 6.0 %all-to-all-done.1.got = f32[8,8,384]{2,1,0:T(8,128)S(1)} async-done(((f32[8,8,384]{2,1,0:T(8,128)}), f32[8,8,384]{2,1,0:T(8,128)S(1)}, u32[]{:S(2)}, u32[]{:S(2)}) %all-to-all-start.1) | async-done | bytes 98336 | tf_op jit(solution)/shard_map/all_to_all | solution.py:489
  46.6 0.7 %place.1 = f32[12,2048]{1,0:T(8,128)} custom-call(f32[8,8,384]{2,1,0:T(8,128)S(1)} %all-to-all-done.1.got), custom_call_target="tpu_custom_call" | custom-call | tf_op jit(solution)/shard_map/place/pallas_call | solution.py:490
  (8 shorter events, 0.1 us)
Async XLA Ops:
  0.6 8.6 %copy-start = (f32[3,12,2048]{2,1,0:T(8,128)S(1)}, f32[3,12,2048]{2,1,0:T(8,128)}, u32[]{:S(2)}) copy-start(f32[3,12,2048]{2,1,0:T(8,128)} %fields.1) | copy-start | bytes 884740
  0.6 8.5 %copy-start.1 = (s32[6,2048]{1,0:T(8,128)S(1)}, s32[6,2048]{1,0:T(8,128)}, u32[]{:S(2)}) copy-start(s32[6,2048]{1,0:T(8,128)} %nbr.5) | copy-start | bytes 147460
  0.7 8.5 %copy-start.2 = (s32[12,1,2048]{2,1,0:T(1,128)S(1)}, s32[12,1,2048]{2,1,0:T(1,128)}, u32[]{:S(2)}) copy-start(s32[12,1,2048]{2,1,0:T(1,128)} %index.3) | copy-start | bytes 294916
  0.7 8.5 %copy-start.3 = (f32[12,1,2048]{2,1,0:T(1,128)S(1)}, f32[12,1,2048]{2,1,0:T(1,128)}, u32[]{:S(2)}) copy-start(f32[12,1,2048]{2,1,0:T(1,128)} %weight.3) | copy-start | bytes 294916
  0.7 8.5 %copy-start.4 = (f32[6,2048]{1,0:T(8,128)S(1)}, f32[6,2048]{1,0:T(8,128)}, u32[]{:S(2)}) copy-start(f32[6,2048]{1,0:T(8,128)} %ex.3) | copy-start | bytes 147460
  0.7 8.5 %copy-start.5 = (f32[6,2048]{1,0:T(8,128)S(1)}, f32[6,2048]{1,0:T(8,128)}, u32[]{:S(2)}) copy-start(f32[6,2048]{1,0:T(8,128)} %ey.3) | copy-start | bytes 147460
  2.7 10.4 %collective-permute-start = (f32[56,768]{1,0:T(8,128)}, f32[56,768]{1,0:T(8,128)S(1)}, u32[]{:S(2)}, u32[]{:S(2)}) collective-permute-start(f32[56,768]{1,0:T(8,128)} %get-tuple-element.19), channel_id=1, source_target_pairs={{0,8},{8,16},{16,24},{24,32},{32,40},{40,48},{48,56},{56,64},{64,7... | collective-permute-start | bytes 516104 | tf_op jit(solution)/shard_map/ppermute | solution.py:440
  2.8 6.4 %copy-start.7 = (f32[1,128]{1,0:T(1,128)S(1)}, f32[1,128]{1,0:T(1,128)}, u32[]{:S(2)}) copy-start(f32[1,128]{1,0:T(1,128)} %get-tuple-element.14.coef_row) | copy-start | bytes 1540
  2.8 10.3 %collective-permute-start.1 = (f32[56,768]{1,0:T(8,128)}, f32[56,768]{1,0:T(8,128)S(1)}, u32[]{:S(2)}, u32[]{:S(2)}) collective-permute-start(f32[56,768]{1,0:T(8,128)} %get-tuple-element.20), channel_id=1, source_target_pairs={{8,0},{16,8},{24,16},{32,24},{40,32},{48,40},{56,48},{64,56},{72,6... | collective-permute-start | bytes 516104 | tf_op jit(solution)/shard_map/ppermute | solution.py:441
  9.2 2.9 %copy-start.9 = (f32[96,96]{1,0:T(8,128)S(1)}, f32[96,96]{1,0:T(8,128)}, u32[]{:S(2)}) copy-start(f32[96,96]{1,0:T(8,128)} %param.17) | copy-start | bytes 110596
  12.2 0.8 %copy-start.8 = (f32[96,96]{1,0:T(8,128)S(1)}, f32[96,96]{1,0:T(8,128)}, u32[]{:S(2)}) copy-start(f32[96,96]{1,0:T(8,128)} %param.18) | copy-start | bytes 110596
  18.6 15.0 %all-to-all-start = ((f32[8,8,1152]{2,1,0:T(8,128)}), f32[8,8,1152]{2,1,0:T(8,128)S(1)}, u32[]{:S(2)}, u32[]{:S(2)}) async-start(f32[8,8,1152]{2,1,0:T(8,128)} %get-tuple-element.22), calls=%async_computation | async-start | bytes 589824 | tf_op jit(solution)/shard_map/all_to_all | solution.py:484
  26.2 0.8 %copy-start.6 = (f32[6,2048]{1,0:T(8,128)S(1)}, f32[6,2048]{1,0:T(8,128)}, u32[]{:S(2)}) copy-start(f32[6,2048]{1,0:T(8,128)} %lap.1) | copy-start | bytes 147460
  35.3 11.2 %all-to-all-start.1 = ((f32[8,8,384]{2,1,0:T(8,128)}), f32[8,8,384]{2,1,0:T(8,128)S(1)}, u32[]{:S(2)}, u32[]{:S(2)}) async-start(f32[8,8,384]{2,1,0:T(8,128)} %solve.1), calls=%async_computation.1 | async-start | bytes 196608 | tf_op jit(solution)/shard_map/all_to_all | solution.py:489

commit v3 on v2

--- a/solution.py
+++ b/solution.py
@@ -21,15 +21,18 @@
 FIELD_EDGE = EDGE + REACH
 WIDE = CELLS + 2 * EDGE
 WIDE_BLOCKS = WIDE // LANES
-CHUNK = CELLS // GROUPS
-WINDOW = CHUNK + 2 * EDGE
+SOLVED = WIDE_BLOCKS - 2
 TILES = 9
 INNER_LO = FIELD_EDGE // LANES
 INNER = (CELLS - 2 * REACH) // LANES
 MATRIX = 8
-HALF = WINDOW // 2
+HALF = WIDE // 2
+SENT = WIDE - LANES
+BANDS = 3
 HALO_ROWS = 56
 COUPLING = 0.5
+
+MIB = 1024 * 1024
 
 f32 = jnp.float32
 bf16 = jnp.bfloat16
@@ -273,26 +276,19 @@
     lax.fori_loop(0, INNER_LO + 1, finish, 0)
 
     lane = lax.broadcasted_iota(jnp.int32, (1, LANES), 1)
-    coef = packed[36:37, 0:LANES]
+    start, end = slice(0, LANES), slice(WIDE - LANES, WIDE)
+    rs[:, start] = jnp.where(lane < NBR_REACH, rs[:, end], rs[:, start])
+    start, end = slice(HALF, HALF + LANES), slice(2 * HALF - LANES, 2 * HALF)
+    rest_rs[0:4, start] = jnp.where(lane < NBR_REACH, rest_rs[4:8, end], rest_rs[0:4, start])
+    rest_rs[4:5, end] = packed[36:37, 0:LANES]
     for j in range(GROUPS):
-        col = j * CHUNK
-        send[j, :, 0:WINDOW] = rs[:, col : col + WINDOW]
-        send[j, :, WINDOW:] = rest_rs[:, HALF + col : 2 * HALF + col]
-        send[j, 0:1, 0:LANES] = jnp.where(lane < NBR_REACH, coef, rs[0:1, col : col + LANES])
-        col = col + WINDOW - LANES
-        send[j, 0:1, WINDOW - LANES : WINDOW] = jnp.where(
-            lane < NBR_REACH, rs[0:1, col : col + LANES], coef
-        )
-
-
-def dot3(a, b):
-    ah, al = a
-    bh, bl = b
-    dot = functools.partial(jnp.dot, preferred_element_type=f32)
-    return dot(ah, bh) + (dot(al, bh) + dot(ah, bl))
-
-
-def band_kernel(group, left, right, nbr, lap, high, low, total, side, side_w):
+        send[j, :, 0:SENT] = rs[:, 0:SENT]
+        send[j, :, SENT:] = rest_rs[:, HALF : 2 * HALF]
+
+
+def band_kernel(left, right, nbr, lap, *refs):
+    *matrices, total, side, side_w = refs
+
     own = lax.broadcasted_iota(jnp.int32, (1, CELLS), 1)
     mid = slice(EDGE, EDGE + CELLS)
     for halo, cells in ((left, slice(0, EDGE)), (right, slice(EDGE + CELLS, WIDE))):
@@ -302,76 +298,101 @@
         side_w[4:6, cells] = halo[54:56, 2 * EDGE :]
     side[:, mid] = nbr[...] - NBR_REACH - own
     side_w[:, mid] = lap[...]
-    start = pl.multiple_of(group[0] * CHUNK, LANES)
-    total[...] = jnp.sum(side_w[:, pl.ds(start, WINDOW)], axis=0, keepdims=True)
+    total[...] = jnp.sum(side_w[...], axis=0, keepdims=True)
     lane = lax.broadcasted_iota(jnp.int32, (1, LANES), 1)
-    slot = lax.broadcasted_iota(jnp.int32, (3 * LANES, LANES), 0)
-    for b in range(4):
-        cells = pl.ds(pl.multiple_of(start + (b + 1) * LANES, LANES), LANES)
-        matrix = jnp.zeros((3 * LANES, LANES), f32)
-        for k in range(SIDES):
-            at = side[k : k + 1, cells] + (lane + LANES)
-            matrix = matrix + jnp.where(slot == at, side_w[k : k + 1, cells], 0.0)
-        high[b], low[b] = split(matrix)
-
-
-def solve_kernel(got, high, low, total, to_first, to_second, from_first, from_second, out):
+    slot = lax.broadcasted_iota(jnp.int32, (2 * LANES, LANES), 0)
+
+    per = SOLVED // BANDS
+    for part, matrix in enumerate(matrices):
+
+        def block(b, carry):
+            cells = pl.ds(pl.multiple_of((part * per + b + 1) * LANES, LANES), LANES)
+            dense = jnp.zeros((2 * LANES, LANES), f32)
+            for k in range(SIDES):
+                at = side[k : k + 1, cells] + (lane + NBR_REACH)
+                dense = dense + jnp.where(slot == at, side_w[k : k + 1, cells], 0.0)
+            high, low = split(dense)
+            matrix[b, :, 0:LANES] = high
+            matrix[b, :, LANES:] = low
+            return carry
+
+        lax.fori_loop(0, per, block, 0)
+
+
+def solve_kernel(
+    got, total, to_first, to_second, from_rows, *refs
+):
+    matrices, (out, x, rhs, scaled, parts, others, last) = refs[:BANDS], refs[BANDS:]
+    per = SOLVED // BANDS
     modes = GROUPS * ROWS
     lane = lax.broadcasted_iota(jnp.int32, (1, LANES), 1)
-    left = got[:, 0, 0:LANES]
-    right = got[:, 0, WINDOW - LANES : WINDOW]
-    coef_row = jnp.sum(jnp.where(lane < NBR_REACH, left, right), axis=0, keepdims=True)
+    coef_row = jnp.sum(got[:, 4, SENT + HALF - LANES :], axis=0, keepdims=True)
     eye = lax.broadcasted_iota(jnp.int32, (modes, LANES), 0) == lax.broadcasted_iota(
         jnp.int32, (modes, LANES), 1
     )
     coef = jnp.sum(jnp.where(eye, coef_row, 0.0), axis=1, keepdims=True)
-    rows = GROUPS * 8
-    main = split(got[:, :, 0:WINDOW].reshape(rows, WINDOW))
-    rest = split(got[:, :, WINDOW:].reshape(rows, HALF))
-    halves = []
-    for matrix, cols in ((to_first, slice(0, HALF)), (to_second, slice(HALF, WINDOW))):
-        levels = tuple(jnp.concatenate([m[:, cols], r], axis=0) for m, r in zip(main, rest))
-        halves.append(dot3(split(matrix[...]), levels))
-    rhs = jnp.concatenate(halves, axis=1)
-    inverse = 1.0 / (1.0 + coef * total[...])
-    rhs = rhs * inverse
-    scaled = coef * inverse
     radius = 6.0 * coef / (1.0 + 6.0 * coef)
     steps = [
         1.0 / (1.0 + radius * math.cos(math.pi * (2 * s + 1) / (2.0 * SWEEPS)))
         for s in range(SWEEPS)
     ]
-    cols = [slice(b * LANES, (b + 1) * LANES) for b in range(6)]
-    iterate = [steps[0] * rhs[:, c] for c in cols]
-    for sweep, blocks in ((1, (1, 2, 3, 4)), (2, (1, 2, 3, 4)), (3, (2, 3))):
-        parts = [jnp.concatenate(split(v), axis=0) for v in iterate]
-        step = steps[sweep]
-        fresh = list(iterate)
-        for b in blocks:
-            near = jnp.concatenate(parts[b - 1 : b + 2], axis=1)
-            both = jnp.concatenate([high[b - 1], low[b - 1]], axis=1)
-            four = jnp.dot(near, both, preferred_element_type=f32)
-            moved = four[:modes, :LANES] + (
-                four[modes:, :LANES] + four[:modes, LANES:] + four[modes:, LANES:]
-            )
-            fresh[b] = (1.0 - step) * iterate[b] + step * (
-                rhs[:, cols[b]] + scaled[:, cols[b]] * moved
-            )
-        iterate = fresh
-    first = dot3(split(from_first[...]), split(iterate[2]))
-    second = dot3(split(from_second[...]), split(iterate[3]))
-    shape = (GROUPS, 8, LANES)
-    out[:, :, 0:LANES] = first[:rows].reshape(shape)
-    out[:, :, LANES:CHUNK] = second[:rows].reshape(shape)
-    out[:, :, CHUNK:] = (first[rows:] + second[rows:]).reshape(shape)
-
-
-def place_kernel(got, out):
-    for j in range(GROUPS):
-        col = j * CHUNK
-        out[0:8, col : col + CHUNK] = got[j, :, 0:CHUNK]
-        out[8:12, col : col + LANES] = got[j, 0:4, CHUNK:]
-        out[8:12, col + LANES : col + CHUNK] = got[j, 4:8, CHUNK:]
+    dot = functools.partial(jnp.dot, preferred_element_type=f32)
+
+    def keep(dst, b, v):
+        both = jnp.concatenate(split(pltpu.roll(v, NBR_REACH, 1)), axis=0)
+        for d in dst:
+            d[b or SOLVED + 1, :, NBR_REACH:] = both[:, NBR_REACH:]
+            d[b + 1, :, 0:NBR_REACH] = both[:, 0:NBR_REACH]
+
+    half = WIDE_BLOCKS // 2
+    transforms = [jnp.concatenate(split(m[...]), axis=0) for m in (to_first, to_second)]
+    for b in range(SOLVED + 1):
+        cols = slice(b * LANES, (b + 1) * LANES)
+        rest = SENT + b % half * LANES
+        levels = jnp.concatenate(
+            [
+                got[:, :, cols].reshape(GROUPS * 8, LANES),
+                got[:, :, rest : rest + LANES].reshape(GROUPS * 8, LANES),
+            ],
+            axis=0,
+        )
+        four = dot(transforms[b // half], jnp.concatenate(split(levels), axis=1))
+        full = four[:modes, :LANES] + (
+            four[modes:, :LANES] + four[:modes, LANES:] + four[modes:, LANES:]
+        )
+        weight = total[:, cols]
+        if b == 0:
+            weight = jnp.where(lane < NBR_REACH, total[:, SENT:], weight)
+        inverse = 1.0 / (1.0 + coef * weight)
+        full = full * inverse
+        rhs[b] = full
+        scaled[b] = coef * inverse
+        full = steps[0] * full
+        x[b] = full
+        keep((parts, others) if b == 0 else (parts,), b, full)
+
+    def swept(source, sweep, b):
+        four = dot(
+            jnp.concatenate([source[b], source[b + 1]], axis=1), matrices[(b - 1) // per][(b - 1) % per]
+        )
+        moved = four[:modes, :LANES] + (
+            four[modes:, :LANES] + four[:modes, LANES:] + four[modes:, LANES:]
+        )
+        return (1.0 - steps[sweep]) * x[b] + steps[sweep] * (rhs[b] + scaled[b] * moved)
+
+    for sweep, source, target in ((1, parts, others), (2, others, parts)):
+        for b in range(1, SOLVED + 1):
+            fresh = swept(source, sweep, b)
+            x[b] = fresh
+            keep((target,), b, fresh)
+    first = EDGE // LANES
+    for i in range(CELLS // LANES):
+        both = jnp.concatenate(split(swept(parts, 3, first + i)), axis=0)
+        last[i // 2, :, i % 2 * LANES : (i % 2 + 1) * LANES] = both
+    back = jnp.concatenate(split(from_rows[...]), axis=0)
+    for i in range(CELLS // (2 * LANES)):
+        both = dot(back, last[i])
+        out[:, 2 * i * LANES : 2 * (i + 1) * LANES] = both[0:ROWS] + both[16 : 16 + ROWS]
 
 
 def slab_order(matrix):
@@ -384,12 +405,11 @@
     ]
 
 
-def call(kernel, outs, scratch=(), name=None, smem=0, n_in=0, space=pltpu.VMEM, vmem=32):
-    in_specs = [pl.BlockSpec(memory_space=pltpu.SMEM)] * smem + [
-        pl.BlockSpec(memory_space=space)
-    ] * (n_in - smem)
+def call(kernel, outs, scratch=(), name=None, spaces="", out_spaces="", vmem=32):
+    kinds = {"s": pltpu.SMEM, "h": pltpu.HBM, "v": pltpu.VMEM}
+    in_specs = [pl.BlockSpec(memory_space=kinds[k]) for k in spaces]
     shapes = [jax.ShapeDtypeStruct(s, d) for s, d in outs]
-    specs = [pl.BlockSpec(memory_space=pltpu.VMEM)] * len(outs)
+    specs = [pl.BlockSpec(memory_space=kinds[k]) for k in out_spaces or "v" * len(outs)]
     if len(outs) == 1:
         shapes, specs = shapes[0], specs[0]
     return pl.pallas_call(
@@ -399,7 +419,7 @@
         out_specs=specs,
         scratch_shapes=list(scratch),
         name=name,
-        compiler_params=pltpu.CompilerParams(vmem_limit_bytes=int(vmem * 1024 * 1024)),
+        compiler_params=pltpu.CompilerParams(vmem_limit_bytes=int(vmem * MIB)),
     )
 
 
@@ -429,10 +449,8 @@
         [halo, halo, ((1, LANES), f32)],
         buffers * 2 + [pltpu.SMEM((ROWS,), f32), pltpu.SemaphoreType.DMA((15,))],
         name="halo",
-        smem=1,
-        n_in=9,
-        space=pltpu.HBM,
-        vmem=62,
+        spaces="s" + 8 * "h",
+        vmem=60,
     )(
         group[None], helm_coef, fields, stencil_index, stencil_weight, neighbours, lap_weight,
         edge_x, edge_y,
@@ -450,11 +468,11 @@
         ],
         [pltpu.VMEM((POINTS, 1, CELLS), jnp.int32), pltpu.VMEM((SIDES, CELLS), jnp.int32)],
         name="inner",
-        n_in=7,
+        spaces=7 * "v",
     )(fields, stencil_index, stencil_weight, neighbours, edge_x, edge_y, coef_row)
     new_winds, send = call(
         outer_kernel,
-        [((2, ROWS, CELLS), f32), ((GROUPS, 8, WINDOW + HALF), f32)],
+        [((2, ROWS, CELLS), f32), ((GROUPS, 8, SENT + HALF), f32)],
         [
             pltpu.VMEM((40, CELLS + 2 * FIELD_EDGE), f32),
             pltpu.VMEM((tiles + 2 * FIELD_EDGE // LANES, 40, 2 * LANES), bf16),
@@ -468,26 +486,35 @@
             pltpu.VMEM((8, WIDE + HALF), f32),
         ],
         name="outer",
-        n_in=11,
+        spaces=11 * "v",
     )(
         packed, slabs, inner, inner_right, left, right, stencil_index, stencil_weight,
         neighbours, edge_x, edge_y,
     )
-    high, low, total = call(
+    bands = ((SOLVED // BANDS, 2 * LANES, 2 * LANES), bf16)
+    *matrices, total = call(
         band_kernel,
-        [((4, 3 * LANES, LANES), bf16), ((4, 3 * LANES, LANES), bf16), ((1, WINDOW), f32)],
+        [bands] * BANDS + [((1, WIDE), f32)],
         [pltpu.VMEM((SIDES, WIDE), jnp.int32), pltpu.VMEM((SIDES, WIDE), f32)],
         name="band",
-        smem=1,
-        n_in=5,
-    )(group[None], left, right, neighbours, lap_weight)
+        spaces=4 * "v",
+    )(left, right, neighbours, lap_weight)
     got = lax.all_to_all(send, "lev", split_axis=0, concat_axis=0, tiled=True)
     to_slabs = [m.T for m in slab_order(to_modes.T)]
-    heights = call(solve_kernel, [((GROUPS, 8, CHUNK + LANES), f32)], name="solve", n_in=8)(
-        got, high, low, total, *to_slabs, *slab_order(from_modes)
-    )
-    heights = lax.all_to_all(heights, "lev", split_axis=0, concat_axis=0, tiled=True)
-    new_height = call(place_kernel, [((ROWS, CELLS), f32)], name="place", n_in=1)(heights)
+    from_rows = lax.dynamic_slice_in_dim(from_modes, group * ROWS, ROWS, 0)
+    from_rows = jnp.pad(jnp.tile(from_rows, (1, 2)), ((0, 16 - ROWS), (0, 0)))
+    modes = GROUPS * ROWS
+    new_height = call(
+        solve_kernel,
+        [((ROWS, CELLS), f32)],
+        [pltpu.VMEM((SOLVED + 1, modes, LANES), f32)] * 3
+        + [pltpu.VMEM((SOLVED + 2, 2 * modes, LANES), bf16)] * 2
+        + [
+            pltpu.VMEM((CELLS // (2 * LANES), 2 * modes, 2 * LANES), bf16),
+        ],
+        name="solve",
+        spaces=(5 + BANDS) * "v",
+    )(got, total, *to_slabs, from_rows, *matrices)
     return new_winds, new_height
 
 

time: 47.6 us -> 43.9 us (0.922)
  the two profiles are of different devices: /device:TPU:2 before, /device:TPU:128 now
where the time goes in v3:
time: 43.9 us; the launch traced here: 43.6 us
  Pallas kernels  16.1 us (37%)
  waiting for transfers between devices  14 us (32%)
  starting transfers between devices  11 us (25%)
  local copies, waits for them, and re-layouts  1.49 us (3%)
  between operations  0.89 us (2%)
    all_to_all x1, waiting for transfers between devices, per_device(): got = lax.all_to_all(send, 'lev', split_axis=0, concat_axis=0, tiled=True)  13.6 us
    all_to_all x1, starting transfers between devices, per_device(): got = lax.all_to_all(send, 'lev', split_axis=0, concat_axis=0, tiled=True)  7.06 us
    pallas_call x1, Pallas kernels, per_device(): call(outer_kernel, [((2, ROWS, CELLS), f32), ((GROUPS, 8, SENT + HALF), f...  5.79 us
    ppermute x1, starting transfers between devices, per_device(): lax.ppermute(head, 'patch', [((i + 1) % patches, i) for i in range(patche...  3.83 us
    pallas_call x1, Pallas kernels, per_device(): call(solve_kernel, [((ROWS, CELLS), f32)], [pltpu.VMEM((SOLVED + 1, modes...  3.34 us
    pallas_call x1, Pallas kernels, per_device(): call(inner_kernel, [((40, CELLS), f32), ((tiles, 40, 2 * LANES), bf16), (...  2.93 us
    pallas_call x1, Pallas kernels, per_device(): call(band_kernel, [bands] * BANDS + [((1, WIDE), f32)], [pltpu.VMEM((SIDE...  2.09 us
    pallas_call x1, Pallas kernels, per_device(): call(halo_kernel, [halo, halo, ((1, LANES), f32)], buffers * 2 + [pltpu.S...  2 us
  transfers between devices with their start and end apart: 3, of which 2 were waited for; matrix products, arithmetic and copies ran while one was open for 3% of the time, Pallas kernels for 12%

profile of v3, /device:TPU:128, one launch (start us, length us, event | category | flops | bytes accessed | tf_op | source)
XLA Modules:
  0.0 43.6 jit_solution(13878924656313780598)
XLA Ops:
  0.6 0.0 copy-start
  0.7 0.0 copy-start.1
  0.7 0.0 copy-start.2
  0.7 0.0 copy-start.3
  0.7 0.0 copy-start.4
  0.7 0.0 copy-start.9
  0.7 0.0 copy-start.10
  0.7 2.0 %halo.1 = (f32[56,768]{1,0:T(8,128)}, f32[56,768]{1,0:T(8,128)}, f32[1,128]{1,0:T(1,128)}) custom-call(s32[1]{0:T(128)} %bitcast.refs_0_, f32[12]{0:T(128)} %refs_1_.1, f32[3,12,2048]{2,1,0:T(8,128)} %fields.1, s32[12,1,2048]{2,1,0:T(1,128)} %index.3, f32[12,1,2048]{2,1,0:T(1,128)} %weight.3, s32[6,2048]{1,0:T(8,128)} %nbr.5, f32[6,2048]{1,0:T(8,128)} %lap.1, ...), custom_call_target="tpu_custom_call" | custom-call | tf_op jit(solution)/shard_map/halo/pallas_call | solution.py:447
  2.7 0.1 collective-permute-start
  2.8 0.0 copy-start.12
  2.8 3.8 %collective-permute-start.1 = (f32[56,768]{1,0:T(8,128)}, f32[56,768]{1,0:T(8,128)S(1)}, u32[]{:S(2)}, u32[]{:S(2)}) collective-permute-start(f32[56,768]{1,0:T(8,128)} %get-tuple-element.21), channel_id=1, source_target_pairs={{8,0},{16,8},{24,16},{32,24},{40,32},{48,40},{56,48},{64,56},{72,6... | collective-permute-start | bytes 516104 | tf_op jit(solution)/shard_map/ppermute | solution.py:459
  6.7 0.0 copy-done.1
  6.7 0.0 copy-done.2
  6.7 0.0 copy-done.3
  6.7 0.0 copy-done.4
  6.7 0.0 copy-done.9
  6.7 0.0 copy-done.10
  6.7 0.0 copy-done.12
  6.7 2.9 %inner.1 = (f32[40,2048]{1,0:T(8,128)S(1)}, bf16[16,40,256]{2,1,0:T(8,128)(2,1)S(1)}, f32[40,1024]{1,0:T(8,128)S(1)}, f32[12,768]{1,0:T(8,128)S(1)}) custom-call(f32[3,12,2048]{2,1,0:T(8,128)S(1)} %copy-done.1, s32[12,1,2048]{2,1,0:T(1,128)S(1)} %copy-done.3, f32[12,1,2048]{2,1,0:T(1,128)S(1)} %copy-done.4, s32[6,2048]{1,0:T(8,128)S(1)} %copy-done.2, ...), custom_call_target="tpu_custom_call" | custom-call | tf_op jit(solution)/shard_map/inner/pallas_call | solution.py:461
  9.6 0.4 collective-permute-done.left
  10.1 0.0 copy-start.5
  10.1 0.0 collective-permute-done.1.right
  10.1 0.0 copy-start.7
  10.1 5.8 %outer.1 = (f32[2,12,2048]{2,1,0:T(8,128)S(1)}, f32[8,8,3712]{2,1,0:T(8,128)}) custom-call(f32[40,2048]{1,0:T(8,128)S(1)} %get-tuple-element.16.packed, bf16[16,40,256]{2,1,0:T(8,128)(2,1)S(1)} %get-tuple-element.17.own_slabs, f32[40,1024]{1,0:T(8,128)S(1)} %get-tuple-element.18.inner, f32[12,768]{1,0:T(8,128)S(1)} %get-tuple-element.19.inner_right, ...), custom_call_target="tpu_custom_call" | custom-call | tf_op jit(solution)/shard_map/outer/pallas_call | solution.py:473
  15.9 0.0 copy-done.5
  15.9 0.0 copy-done.7
  15.9 0.0 copy-start.13
  15.9 7.1 %all-to-all-start = ((f32[8,8,3712]{2,1,0:T(8,128)}), f32[8,8,3712]{2,1,0:T(8,128)S(1)}, u32[]{:S(2)}, u32[]{:S(2)}) async-start(f32[8,8,3712]{2,1,0:T(8,128)} %get-tuple-element.23), calls=%async_computation | async-start | bytes 1900544 | tf_op jit(solution)/shard_map/all_to_all | solution.py:502
  22.9 0.0 copy-done.13
  22.9 0.1 copy.13
  23.1 0.1 copy.17
  23.2 0.1 copy.14
  23.3 0.1 copy.15
  23.3 0.0 copy-done
  23.4 0.1 tile.10
  23.5 0.1 maximum_bitcast_fusion.1
  23.6 0.0 copy-start.6
  23.6 0.0 copy-start.8
  23.6 0.0 copy-start.11
  23.6 0.8 %copy.18 = f32[2,12,2048]{2,0,1:T(2,128)} copy(f32[2,12,2048]{2,1,0:T(8,128)S(1)} %get-tuple-element.30) | data formatting | bytes 393216
  24.4 0.1 copy-done.6
  24.5 0.1 copy-done.8
  24.6 0.0 copy-done.11
  24.6 2.1 %band.1 = (bf16[6,256,256]{2,1,0:T(8,128)(2,1)S(1)}, bf16[6,256,256]{2,1,0:T(8,128)(2,1)S(1)}, bf16[6,256,256]{2,1,0:T(8,128)(2,1)S(1)}, f32[1,2560]{1,0:T(1,128)S(1)}) custom-call(f32[56,768]{1,0:T(8,128)S(1)} %copy-done.6, f32[56,768]{1,0:T(8,128)S(1)} %copy-done.8, s32[6,2048]{1,0:T(8,128)S(1)} %copy-done.2, f32[6,2048]{1,0:T(8,128)S(1)} %copy-done.11), custom_call_target="tpu_custom_call" | custom-call | tf_op jit(solution)/shard_map/band/pallas_call | solution.py:495
  26.7 13.6 %all-to-all-done.got = f32[8,8,3712]{2,1,0:T(8,128)S(1)} async-done(((f32[8,8,3712]{2,1,0:T(8,128)}), f32[8,8,3712]{2,1,0:T(8,128)S(1)}, u32[]{:S(2)}, u32[]{:S(2)}) %all-to-all-start) | async-done | bytes 950304 | tf_op jit(solution)/shard_map/all_to_all | solution.py:502
  40.3 3.3 %solve.1 = f32[12,2048]{1,0:T(8,128)} custom-call(f32[8,8,3712]{2,1,0:T(8,128)S(1)} %all-to-all-done.got, f32[1,2560]{1,0:T(1,128)S(1)} %get-tuple-element.24.total, f32[96,128]{1,0:T(8,128)S(1)} %get-tuple-element.33.to_first, f32[96,128]{1,0:T(8,128)S(1)} %get-tuple-element.32.to_second, f32[16,192]{1,0:T(8,128)S(1)} %pad.14.from_rows, ...), custom_call_target="tpu_custom_call" | custom-call | tf_op jit(solution)/shard_map/solve/pallas_call | solution.py:507
  (7 shorter events, 0.1 us)
Async XLA Ops:
  0.6 22.7 %copy-start = (f32[96,96]{1,0:T(8,128)S(1)}, f32[96,96]{1,0:T(8,128)}, u32[]{:S(2)}) copy-start(f32[96,96]{1,0:T(8,128)} %param.18) | copy-start | bytes 110596
  0.7 6.0 %copy-start.1 = (f32[3,12,2048]{2,1,0:T(8,128)S(1)}, f32[3,12,2048]{2,1,0:T(8,128)}, u32[]{:S(2)}) copy-start(f32[3,12,2048]{2,1,0:T(8,128)} %fields.1) | copy-start | bytes 884740
  0.7 6.0 %copy-start.2 = (s32[6,2048]{1,0:T(8,128)S(1)}, s32[6,2048]{1,0:T(8,128)}, u32[]{:S(2)}) copy-start(s32[6,2048]{1,0:T(8,128)} %nbr.5) | copy-start | bytes 147460
  0.7 6.0 %copy-start.3 = (s32[12,1,2048]{2,1,0:T(1,128)S(1)}, s32[12,1,2048]{2,1,0:T(1,128)}, u32[]{:S(2)}) copy-start(s32[12,1,2048]{2,1,0:T(1,128)} %index.3) | copy-start | bytes 294916
  0.7 6.0 %copy-start.4 = (f32[12,1,2048]{2,1,0:T(1,128)S(1)}, f32[12,1,2048]{2,1,0:T(1,128)}, u32[]{:S(2)}) copy-start(f32[12,1,2048]{2,1,0:T(1,128)} %weight.3) | copy-start | bytes 294916
  0.7 6.0 %copy-start.9 = (f32[6,2048]{1,0:T(8,128)S(1)}, f32[6,2048]{1,0:T(8,128)}, u32[]{:S(2)}) copy-start(f32[6,2048]{1,0:T(8,128)} %ex.3) | copy-start | bytes 147460
  0.7 6.0 %copy-start.10 = (f32[6,2048]{1,0:T(8,128)S(1)}, f32[6,2048]{1,0:T(8,128)}, u32[]{:S(2)}) copy-start(f32[6,2048]{1,0:T(8,128)} %ey.3) | copy-start | bytes 147460
  2.7 7.3 %collective-permute-start = (f32[56,768]{1,0:T(8,128)}, f32[56,768]{1,0:T(8,128)S(1)}, u32[]{:S(2)}, u32[]{:S(2)}) collective-permute-start(f32[56,768]{1,0:T(8,128)} %get-tuple-element.20), channel_id=1, source_target_pairs={{0,8},{8,16},{16,24},{24,32},{32,40},{40,48},{48,56},{56,64},{64,7... | collective-permute-start | bytes 516104 | tf_op jit(solution)/shard_map/ppermute | solution.py:458
  2.8 3.9 %copy-start.12 = (f32[1,128]{1,0:T(1,128)S(1)}, f32[1,128]{1,0:T(1,128)}, u32[]{:S(2)}) copy-start(f32[1,128]{1,0:T(1,128)} %get-tuple-element.15.coef_row) | copy-start | bytes 1540
  2.8 7.2 %collective-permute-start.1 = (f32[56,768]{1,0:T(8,128)}, f32[56,768]{1,0:T(8,128)S(1)}, u32[]{:S(2)}, u32[]{:S(2)}) collective-permute-start(f32[56,768]{1,0:T(8,128)} %get-tuple-element.21), channel_id=1, source_target_pairs={{8,0},{16,8},{24,16},{32,24},{40,32},{48,40},{56,48},{64,56},{72,6... | collective-permute-start | bytes 516104 | tf_op jit(solution)/shard_map/ppermute | solution.py:459
  10.1 5.8 %copy-start.5 = (f32[56,768]{1,0:T(8,128)}, f32[56,768]{1,0:T(8,128)S(1)}, u32[]{:S(2)}) copy-start(f32[56,768]{1,0:T(8,128)S(1)} %collective-permute-done.left) | copy-start | bytes 516100
  10.1 5.8 %copy-start.7 = (f32[56,768]{1,0:T(8,128)}, f32[56,768]{1,0:T(8,128)S(1)}, u32[]{:S(2)}) copy-start(f32[56,768]{1,0:T(8,128)S(1)} %collective-permute-done.1.right) | copy-start | bytes 516100
  15.9 7.1 %copy-start.13 = (f32[96,96]{1,0:T(8,128)S(1)}, f32[96,96]{1,0:T(8,128)}, u32[]{:S(2)}) copy-start(f32[96,96]{1,0:T(8,128)} %param.17) | copy-start | bytes 110596
  15.9 24.4 %all-to-all-start = ((f32[8,8,3712]{2,1,0:T(8,128)}), f32[8,8,3712]{2,1,0:T(8,128)S(1)}, u32[]{:S(2)}, u32[]{:S(2)}) async-start(f32[8,8,3712]{2,1,0:T(8,128)} %get-tuple-element.23), calls=%async_computation | async-start | bytes 1900544 | tf_op jit(solution)/shard_map/all_to_all | solution.py:502
  23.6 0.9 %copy-start.6 = (f32[56,768]{1,0:T(8,128)S(1)}, f32[56,768]{1,0:T(8,128)}, u32[]{:S(2)}) copy-start(f32[56,768]{1,0:T(8,128)} %copy-done.5) | copy-start | bytes 516100
  23.6 1.0 %copy-start.8 = (f32[56,768]{1,0:T(8,128)S(1)}, f32[56,768]{1,0:T(8,128)}, u32[]{:S(2)}) copy-start(f32[56,768]{1,0:T(8,128)} %copy-done.7) | copy-start | bytes 516100
  23.6 1.0 %copy-start.11 = (f32[6,2048]{1,0:T(8,128)S(1)}, f32[6,2048]{1,0:T(8,128)}, u32[]{:S(2)}) copy-start(f32[6,2048]{1,0:T(8,128)} %lap.1) | copy-start | bytes 147460

commit v4 on v3

--- a/solution.py
+++ b/solution.py
@@ -28,7 +28,7 @@
 MATRIX = 8
 HALF = WIDE // 2
 SENT = WIDE - LANES
-BANDS = 3
+BANDS = 6
 HALO_ROWS = 56
 COUPLING = 0.5
 
@@ -96,25 +96,27 @@
         dst[first + t, :, LANES:] = low
 
 
-def stencil_block(x, slabs, first, col, away, weight, away_col):
+def stencil_block(x, col, slabs, slab, first, count, away, weight, matrix):
     groups = 5
     acc = [jnp.zeros((8, LANES), f32) for _ in range(groups)]
     lane = lax.broadcasted_iota(jnp.int32, (1, LANES), 1)
     slot = lax.broadcasted_iota(jnp.int32, (LANES, LANES), 0).astype(bf16)
     ones = jnp.ones((LANES, LANES), bf16)
-    near = slabs[pl.ds(first, TILES)].reshape(TILES * 8 * groups, 2 * LANES)
+    if matrix:
+        near = slabs[pl.ds(slab, count)].reshape(count * 8 * groups, 2 * LANES)
 
     def locate(p):
-        at = away[p, :, pl.ds(away_col, LANES)] + (lane + REACH)
-        w = jnp.broadcast_to(weight[p, :, pl.ds(away_col, LANES)], (8, LANES))
+        at = away(p) + (lane + REACH)
+        w = jnp.broadcast_to(weight(p), (8, LANES))
         return at & (LANES - 1), jnp.broadcast_to(at >> 7, (8, LANES)), w
 
     def add(part, tile, w):
-        picked = [None] * groups
-        for t in range(TILES):
-            mask = tile == t
+        picked = [None if count == TILES else jnp.zeros((8, LANES), f32)] * groups
+        for t in range(count):
+            mask = tile == first + t
             for g in range(groups):
-                picked[g] = part(t, g) if t == 0 else jnp.where(mask, part(t, g), picked[g])
+                value = part(t, g)
+                picked[g] = value if picked[g] is None else jnp.where(mask, value, picked[g])
         for g in range(groups):
             acc[g] = acc[g] + w * picked[g]
 
@@ -132,8 +134,8 @@
 
         add(part, tile, w)
 
-    plain = list(range(MATRIX, POINTS))
-    for pair in range(0, MATRIX, 2):
+    plain = list(range(matrix, POINTS))
+    for pair in range(0, matrix, 2):
         points = [locate(p) for p in (pair, pair + 1)]
         hot = jnp.concatenate([one_hot(inside) for inside, _, _ in points], axis=1)
         rows = jnp.dot(near, jnp.concatenate([hot, hot], axis=0), preferred_element_type=f32)
@@ -145,6 +147,12 @@
     for p in plain:
         gathered(p)
     return acc
+
+
+def own_points(index, weight, col):
+    own = lax.broadcasted_iota(jnp.int32, (1, LANES), 1) + (col + REACH)
+    cells = pl.ds(col, LANES)
+    return lambda p: index[p, :, cells] - own, lambda p: weight[p, :, cells]
 
 
 def right_side_block(up, up_col, side, side_x, side_y, col):
@@ -174,84 +182,102 @@
 
 def inner_kernel(
     fields, index, weight, nbr, ex, ey, coef_row,
-    packed, slabs, upstream, right, away, side,
+    packed, slabs, upstream, right, side,
 ):
     pack_fields(packed, 0, fields, 0, CELLS)
     packed[36:37, 0:LANES] = coef_row[...]
     split_tiles(slabs, 0, packed, 0, CELLS // LANES)
     own = lax.broadcasted_iota(jnp.int32, (1, CELLS), 1)
-    for p in range(POINTS):
-        away[p] = index[p] - REACH - own
     side[...] = nbr[...] - NBR_REACH - own
-
-    def stencil(b, carry):
-        col = pl.multiple_of(b * LANES, LANES)
+    tiles = CELLS // LANES
+    reach = REACH // LANES
+
+    def block(b, tile, first, count):
+        col = b * LANES if isinstance(b, int) else pl.multiple_of(b * LANES, LANES)
+        start = tile * LANES if isinstance(b, int) else pl.multiple_of(tile * LANES, LANES)
+        away, points_weight = own_points(index, weight, col)
         acc = stencil_block(
-            packed, slabs, b, col, away, weight, pl.multiple_of(col + REACH, LANES)
+            packed, start, slabs, tile, first, count, away, points_weight, MATRIX
         )
         for g in range(5):
             upstream[8 * g : 8 * g + 8, pl.ds(col, LANES)] = acc[g]
+
+    def whole(i, carry):
+        block(i + reach, i, 0, TILES)
         return carry
 
-    lax.fori_loop(0, INNER, stencil, 0, unroll=4)
+    lax.fori_loop(0, INNER, whole, 0, unroll=4)
 
     def finish(b, carry):
-        col = pl.multiple_of(b * LANES, LANES)
-        top, rest = right_side_block(
-            upstream, col, side, ex, ey, pl.multiple_of(col + REACH + LANES, LANES)
-        )
-        right[0:8, pl.ds(col, LANES)] = top
-        right[8:12, pl.ds(col, LANES)] = rest
+        col = pl.multiple_of((b + reach) * LANES, LANES)
+        cells = pl.multiple_of(col + LANES, LANES)
+        top, rest = right_side_block(upstream, col, side, ex, ey, cells)
+        right[0:8, pl.ds(b * LANES, LANES)] = top
+        right[8:12, pl.ds(b * LANES, LANES)] = rest
         return carry
 
     lax.fori_loop(0, INNER - 2, finish, 0, unroll=2)
+    for b in range(reach):
+        block(b, 0, reach - b, reach + 1 + b)
+        block(tiles - 1 - b, tiles - 1 - b - reach, 0, reach + 1 + b)
 
 
 def outer_kernel(
-    packed, own_slabs, inner, inner_right, left, right, index, weight, nbr, ex, ey,
-    winds, send, x, slabs, up, away, w_all, side, side_x, side_y, rs, rest_rs,
+    packed, own_slabs, inner, inner_right, left, right, index, weight, own_side, ex, ey,
+    winds, send, x, slabs, up, side, side_x, side_y, rs, rest_rs,
 ):
     halo_tiles = FIELD_EDGE // LANES
-    x[:, 0:FIELD_EDGE] = left[0:40, :]
-    x[:, FIELD_EDGE : FIELD_EDGE + CELLS] = packed[...]
-    x[:, FIELD_EDGE + CELLS :] = right[0:40, :]
-    split_tiles(slabs, 0, left, 0, halo_tiles)
-    slabs[halo_tiles : halo_tiles + CELLS // LANES] = own_slabs[...]
-    split_tiles(slabs, halo_tiles + CELLS // LANES, right, 0, halo_tiles)
-    own = lax.broadcasted_iota(jnp.int32, (1, CELLS), 1)
+    reach = REACH // LANES
+    edge = EDGE // LANES
+    x[0, :, 0:FIELD_EDGE] = left[0:40, :]
+    x[0, :, FIELD_EDGE:] = packed[:, 0:REACH]
+    x[1, :, 0:REACH] = packed[:, CELLS - REACH :]
+    x[1, :, REACH:] = right[0:40, :]
+    split_tiles(slabs.at[0], 0, left, 0, halo_tiles)
+    slabs[0, halo_tiles:] = own_slabs[0:reach]
+    slabs[1, 0:reach] = own_slabs[CELLS // LANES - reach :]
+    split_tiles(slabs.at[1], reach, right, 0, halo_tiles)
     mid = slice(EDGE, EDGE + CELLS)
     for halo, cells in ((left, slice(0, EDGE)), (right, slice(EDGE + CELLS, WIDE))):
-        for p in range(POINTS):
-            away[p, :, cells] = halo[40 + p : 41 + p, 0:EDGE].astype(jnp.int32)
-            w_all[p, :, cells] = halo[40 + p : 41 + p, EDGE : 2 * EDGE]
         side[0:4, cells] = halo[52:56, 0:EDGE].astype(jnp.int32)
         side[4:6, cells] = halo[52:54, 2 * EDGE :].astype(jnp.int32)
         side_x[:, cells] = halo[40:46, 2 * EDGE :]
         side_y[:, cells] = halo[46:52, 2 * EDGE :]
-    for start in (0, CELLS - REACH):
-        there = start + lax.broadcasted_iota(jnp.int32, (1, REACH), 1)
-        cells = slice(EDGE + start, EDGE + start + REACH)
-        for p in range(POINTS):
-            away[p, :, cells] = index[p, :, start : start + REACH] - REACH - there
-            w_all[p, :, cells] = weight[p, :, start : start + REACH]
-    side[:, mid] = nbr[...] - NBR_REACH - own
+    side[:, mid] = own_side[...]
     side_x[:, mid] = ex[...]
     side_y[:, mid] = ey[...]
 
     up[:, 0:LANES] = jnp.zeros((40, LANES), f32)
     up[:, LANES + WIDE :] = jnp.zeros((40, LANES), f32)
-    first = LANES * (1 + INNER_LO)
-    up[:, first : first + INNER * LANES] = inner[...]
-
-    def stencil(i, carry):
-        for b in (i, i + INNER_LO + INNER):
-            col = pl.multiple_of(b * LANES, LANES)
-            acc = stencil_block(x, slabs, b, col, away, w_all, col)
+    up[:, LANES + EDGE : LANES + EDGE + CELLS] = inner[...]
+
+    def halo_points(halo, col):
+        cells = slice(col, col + LANES)
+        far = slice(EDGE + col, EDGE + col + LANES)
+        return (
+            lambda p: halo[40 + p : 41 + p, cells].astype(jnp.int32),
+            lambda p: halo[40 + p : 41 + p, far],
+        )
+
+    for b in range(halo_tiles):
+        for s, halo in ((0, left), (1, right)):
+            if b < edge:
+                at = b if s == 0 else WIDE_BLOCKS - edge + b
+                points = halo_points(halo, b * LANES)
+                tile, first, count = b, 0, TILES
+            else:
+                count = halo_tiles - b
+                at = b if s == 0 else WIDE_BLOCKS - 1 - b
+                points = own_points(index, weight, (at - edge) * LANES)
+                tile, first = (b, 0) if s == 0 else (reach, TILES - count)
+            acc = stencil_block(
+                x.at[s], tile * LANES, slabs.at[s], tile, first, count, *points,
+                MATRIX if count > 2 else 0,
+            )
+            cells = slice((at + 1) * LANES, (at + 2) * LANES)
             for g in range(5):
-                up[8 * g : 8 * g + 8, pl.ds(col + LANES, LANES)] = acc[g]
-        return carry
-
-    lax.fori_loop(0, INNER_LO, stencil, 0, unroll=3)
+                rows = slice(8 * g, 8 * g + 8)
+                up[rows, cells] = acc[g] if b < edge else up[rows, cells] + acc[g]
 
     for field in range(2):
         cells = slice(LANES + EDGE, LANES + EDGE + CELLS)
@@ -458,27 +484,26 @@
     left = lax.ppermute(tail, "patch", [(i, (i + 1) % patches) for i in range(patches)])
     right = lax.ppermute(head, "patch", [((i + 1) % patches, i) for i in range(patches)])
     tiles = CELLS // LANES
-    packed, slabs, inner, inner_right = call(
+    packed, slabs, inner, inner_right, side = call(
         inner_kernel,
         [
             ((40, CELLS), f32),
             ((tiles, 40, 2 * LANES), bf16),
-            ((40, INNER * LANES), f32),
+            ((40, CELLS), f32),
             ((ROWS, (INNER - 2) * LANES), f32),
+            ((SIDES, CELLS), jnp.int32),
         ],
-        [pltpu.VMEM((POINTS, 1, CELLS), jnp.int32), pltpu.VMEM((SIDES, CELLS), jnp.int32)],
         name="inner",
         spaces=7 * "v",
     )(fields, stencil_index, stencil_weight, neighbours, edge_x, edge_y, coef_row)
+    near = (FIELD_EDGE + REACH) // LANES
     new_winds, send = call(
         outer_kernel,
         [((2, ROWS, CELLS), f32), ((GROUPS, 8, SENT + HALF), f32)],
         [
-            pltpu.VMEM((40, CELLS + 2 * FIELD_EDGE), f32),
-            pltpu.VMEM((tiles + 2 * FIELD_EDGE // LANES, 40, 2 * LANES), bf16),
+            pltpu.VMEM((2, 40, near * LANES), f32),
+            pltpu.VMEM((2, near, 40, 2 * LANES), bf16),
             pltpu.VMEM((40, WIDE + 2 * LANES), f32),
-            pltpu.VMEM((POINTS, 1, WIDE), jnp.int32),
-            pltpu.VMEM((POINTS, 1, WIDE), f32),
             pltpu.VMEM((SIDES, WIDE), jnp.int32),
             pltpu.VMEM((SIDES, WIDE), f32),
             pltpu.VMEM((SIDES, WIDE), f32),
@@ -489,7 +514,7 @@
         spaces=11 * "v",
     )(
         packed, slabs, inner, inner_right, left, right, stencil_index, stencil_weight,
-        neighbours, edge_x, edge_y,
+        side, edge_x, edge_y,
     )
     bands = ((SOLVED // BANDS, 2 * LANES, 2 * LANES), bf16)
     *matrices, total = call(

time: 43.9 us -> 43.7 us (level)
  waiting for transfers between devices: 14 us -> 12.1 us
  local copies, waits for them, and re-layouts: 1.49 us -> 3.09 us
    unnamed x29 -> x25, local copies, waits for them, and re-layouts: 1.03 us -> 2.62 us
    all_to_all x1, waiting for transfers between devices: 13.6 us -> 12.1 us  [per_device(): got = lax.all_to_all(send, 'lev', split_axis=0, concat_axis=0, tiled=True)]
    pallas_call x1, Pallas kernels: 2.93 us -> 4.17 us  [per_device(): call(inner_kernel, [((40, CELLS), f32), ((tiles, 40, 2 * LANES), bf16), (...]
    pallas_call x1, Pallas kernels: 5.79 us -> 4.59 us  [per_device(): call(outer_kernel, [((2, ROWS, CELLS), f32), ((GROUPS, 8, SENT + HALF), f...]
  transfers between devices with their start and end apart: 3 -> 3, of which waited for: 2 -> 1; matrix products, arithmetic and copies ran while one was open for 3% -> 3% of each run, Pallas kernels for 12% -> 15%
where the time goes in v4:
time: 43.7 us; the launch traced here: 43.4 us
  Pallas kernels  16.2 us (37%)
  waiting for transfers between devices  12.1 us (28%)
  starting transfers between devices  11 us (25%)
  local copies, waits for them, and re-layouts  3.09 us (7%)
  between operations  0.89 us (2%)
    all_to_all x1, waiting for transfers between devices, per_device(): got = lax.all_to_all(send, 'lev', split_axis=0, concat_axis=0, tiled=True)  12.1 us
    all_to_all x1, starting transfers between devices, per_device(): got = lax.all_to_all(send, 'lev', split_axis=0, concat_axis=0, tiled=True)  7.06 us
    pallas_call x1, Pallas kernels, per_device(): call(outer_kernel, [((2, ROWS, CELLS), f32), ((GROUPS, 8, SENT + HALF), f...  4.59 us
    pallas_call x1, Pallas kernels, per_device(): call(inner_kernel, [((40, CELLS), f32), ((tiles, 40, 2 * LANES), bf16), (...  4.17 us
    ppermute x1, starting transfers between devices, per_device(): lax.ppermute(head, 'patch', [((i + 1) % patches, i) for i in range(patche...  3.83 us
    pallas_call x1, Pallas kernels, per_device(): call(solve_kernel, [((ROWS, CELLS), f32)], [pltpu.VMEM((SOLVED + 1, modes...  3.33 us
    unnamed x25, local copies, waits for them, and re-layouts  2.62 us
    pallas_call x1, Pallas kernels, per_device(): call(band_kernel, [bands] * BANDS + [((1, WIDE), f32)], [pltpu.VMEM((SIDE...  2.16 us
  transfers between devices with their start and end apart: 3, of which 1 were waited for; matrix products, arithmetic and copies ran while one was open for 3% of the time, Pallas kernels for 15%

profile of v4, /device:TPU:128, one launch (start us, length us, event | category | flops | bytes accessed | tf_op | source)
XLA Modules:
  0.0 43.4 jit_solution(4644436737844462039)
XLA Ops:
  0.6 0.0 copy-start
  0.7 0.0 copy-start.1
  0.7 0.0 copy-start.2
  0.7 0.0 copy-start.3
  0.7 0.0 copy-start.4
  0.7 0.0 copy-start.5
  0.7 0.0 copy-start.6
  0.7 2.0 %halo.1 = (f32[56,768]{1,0:T(8,128)}, f32[56,768]{1,0:T(8,128)}, f32[1,128]{1,0:T(1,128)}) custom-call(s32[1]{0:T(128)} %bitcast.refs_0_, f32[12]{0:T(128)} %refs_1_.1, f32[3,12,2048]{2,1,0:T(8,128)} %fields.1, s32[12,1,2048]{2,1,0:T(1,128)} %index.3, f32[12,1,2048]{2,1,0:T(1,128)} %weight.3, s32[6,2048]{1,0:T(8,128)} %nbr.3, f32[6,2048]{1,0:T(8,128)} %lap.1, ...), custom_call_target="tpu_custom_call" | custom-call | tf_op jit(solution)/shard_map/halo/pallas_call | solution.py:473
  2.7 0.1 collective-permute-start
  2.8 0.0 copy-start.10
  2.8 3.8 %collective-permute-start.1 = (f32[56,768]{1,0:T(8,128)}, f32[56,768]{1,0:T(8,128)S(1)}, u32[]{:S(2)}, u32[]{:S(2)}) collective-permute-start(f32[56,768]{1,0:T(8,128)} %get-tuple-element.25), channel_id=1, source_target_pairs={{8,0},{16,8},{24,16},{32,24},{40,32},{48,40},{56,48},{64,56},{72,6... | collective-permute-start | bytes 516104 | tf_op jit(solution)/shard_map/ppermute | solution.py:485
  6.7 0.0 copy-done.1
  6.7 0.0 copy-done.2
  6.7 0.0 copy-done.3
  6.7 0.0 copy-done.4
  6.7 0.0 copy-done.5
  6.7 0.0 copy-done.6
  6.7 0.0 copy-done.10
  6.7 4.2 %inner.1 = (f32[40,2048]{1,0:T(8,128)S(1)}, bf16[16,40,256]{2,1,0:T(8,128)(2,1)S(1)}, f32[40,2048]{1,0:T(8,128)S(1)}, f32[12,768]{1,0:T(8,128)S(1)}, s32[6,2048]{1,0:T(8,128)S(1)}) custom-call(f32[3,12,2048]{2,1,0:T(8,128)S(1)} %copy-done.1, s32[12,1,2048]{2,1,0:T(1,128)S(1)} %copy-done.2, f32[12,1,2048]{2,1,0:T(1,128)S(1)} %copy-done.3, ...), custom_call_target="tpu_custom_call" | custom-call | tf_op jit(solution)/shard_map/inner/pallas_call | solution.py:487
  10.9 0.0 collective-permute-done.left
  10.9 0.0 collective-permute-done.1.right
  10.9 4.6 %outer.1 = (f32[2,12,2048]{2,1,0:T(8,128)S(1)}, f32[8,8,3712]{2,1,0:T(8,128)}) custom-call(f32[40,2048]{1,0:T(8,128)S(1)} %get-tuple-element.20.packed, bf16[16,40,256]{2,1,0:T(8,128)(2,1)S(1)} %get-tuple-element.21.own_slabs, f32[40,2048]{1,0:T(8,128)S(1)} %get-tuple-element.22.inner, f32[12,768]{1,0:T(8,128)S(1)} %get-tuple-element.23.inner_right, ...), custom_call_target="tpu_custom_call" | custom-call | tf_op jit(solution)/shard_map/outer/pallas_call | solution.py:500
  15.5 0.0 copy-start.11
  15.5 7.1 %all-to-all-start = ((f32[8,8,3712]{2,1,0:T(8,128)}), f32[8,8,3712]{2,1,0:T(8,128)S(1)}, u32[]{:S(2)}, u32[]{:S(2)}) async-start(f32[8,8,3712]{2,1,0:T(8,128)} %get-tuple-element.28), calls=%async_computation | async-start | bytes 1900544 | tf_op jit(solution)/shard_map/all_to_all | solution.py:527
  22.5 0.0 copy-done.11
  22.5 0.1 copy.13
  22.7 0.1 copy.17
  22.8 0.1 copy.14
  22.9 0.1 copy.15
  23.0 0.0 copy-done
  23.0 0.1 tile.10
  23.1 0.1 maximum_bitcast_fusion.1
  23.2 0.0 copy-start.9
  23.2 0.8 %copy.18 = f32[2,12,2048]{2,0,1:T(2,128)} copy(f32[2,12,2048]{2,1,0:T(8,128)S(1)} %get-tuple-element.38) | data formatting | bytes 393216
  24.0 0.0 copy-done.9
  24.0 2.2 %band.1 = (bf16[3,256,256]{2,1,0:T(8,128)(2,1)S(1)}, bf16[3,256,256]{2,1,0:T(8,128)(2,1)S(1)}, bf16[3,256,256]{2,1,0:T(8,128)(2,1)S(1)}, bf16[3,256,256]{2,1,0:T...) custom-call(f32[56,768]{1,0:T(8,128)S(1)} %collective-permute-done.left,, ...), custom_call_target="tpu_custom_call" | custom-call | tf_op jit(solution)/shard_map/band/pallas_call | solution.py:520
  26.2 0.0 copy-start.7
  26.2 0.7 %copy-done.7 = bf16[3,256,256]{2,1,0:T(8,128)(2,1)} copy-done((bf16[3,256,256]{2,1,0:T(8,128)(2,1)}, bf16[3,256,256]{2,1,0:T(8,128)(2,1)S(1)}, u32[]{:S(2)}) %copy-start.7) | copy-done | bytes 393240
  27.0 12.1 %all-to-all-done.got = f32[8,8,3712]{2,1,0:T(8,128)S(1)} async-done(((f32[8,8,3712]{2,1,0:T(8,128)}), f32[8,8,3712]{2,1,0:T(8,128)S(1)}, u32[]{:S(2)}, u32[]{:S(2)}) %all-to-all-start) | async-done | bytes 950304 | tf_op jit(solution)/shard_map/all_to_all | solution.py:527
  39.0 0.0 copy-start.8
  39.0 1.0 %copy-done.8 = bf16[3,256,256]{2,1,0:T(8,128)(2,1)S(1)} copy-done((bf16[3,256,256]{2,1,0:T(8,128)(2,1)S(1)}, bf16[3,256,256]{2,1,0:T(8,128)(2,1)}, u32[]{:S(2)}) %copy-start.8) | copy-done | bytes 393240
  40.0 3.3 %solve.1 = f32[12,2048]{1,0:T(8,128)} custom-call(f32[8,8,3712]{2,1,0:T(8,128)S(1)} %all-to-all-done.got, f32[1,2560]{1,0:T(1,128)S(1)} %get-tuple-element.29.total, f32[96,128]{1,0:T(8,128)S(1)} %get-tuple-element.41.to_first, f32[96,128]{1,0:T(8,128)S(1)} %get-tuple-element.40.to_second, f32[16,192]{1,0:T(8,128)S(1)} %pad.14.from_rows, ...), custom_call_target="tpu_custom_call" | custom-call | tf_op jit(solution)/shard_map/solve/pallas_call | solution.py:532
  (7 shorter events, 0.1 us)
Async XLA Ops:
  0.6 22.3 %copy-start = (f32[96,96]{1,0:T(8,128)S(1)}, f32[96,96]{1,0:T(8,128)}, u32[]{:S(2)}) copy-start(f32[96,96]{1,0:T(8,128)} %param.18) | copy-start | bytes 110596
  0.7 6.0 %copy-start.1 = (f32[3,12,2048]{2,1,0:T(8,128)S(1)}, f32[3,12,2048]{2,1,0:T(8,128)}, u32[]{:S(2)}) copy-start(f32[3,12,2048]{2,1,0:T(8,128)} %fields.1) | copy-start | bytes 884740
  0.7 6.0 %copy-start.2 = (s32[12,1,2048]{2,1,0:T(1,128)S(1)}, s32[12,1,2048]{2,1,0:T(1,128)}, u32[]{:S(2)}) copy-start(s32[12,1,2048]{2,1,0:T(1,128)} %index.3) | copy-start | bytes 294916
  0.7 6.0 %copy-start.3 = (f32[12,1,2048]{2,1,0:T(1,128)S(1)}, f32[12,1,2048]{2,1,0:T(1,128)}, u32[]{:S(2)}) copy-start(f32[12,1,2048]{2,1,0:T(1,128)} %weight.3) | copy-start | bytes 294916
  0.7 6.0 %copy-start.4 = (f32[6,2048]{1,0:T(8,128)S(1)}, f32[6,2048]{1,0:T(8,128)}, u32[]{:S(2)}) copy-start(f32[6,2048]{1,0:T(8,128)} %ex.3) | copy-start | bytes 147460
  0.7 6.0 %copy-start.5 = (f32[6,2048]{1,0:T(8,128)S(1)}, f32[6,2048]{1,0:T(8,128)}, u32[]{:S(2)}) copy-start(f32[6,2048]{1,0:T(8,128)} %ey.3) | copy-start | bytes 147460
  0.7 6.0 %copy-start.6 = (s32[6,2048]{1,0:T(8,128)S(1)}, s32[6,2048]{1,0:T(8,128)}, u32[]{:S(2)}) copy-start(s32[6,2048]{1,0:T(8,128)} %nbr.3) | copy-start | bytes 147460
  2.7 8.2 %collective-permute-start = (f32[56,768]{1,0:T(8,128)}, f32[56,768]{1,0:T(8,128)S(1)}, u32[]{:S(2)}, u32[]{:S(2)}) collective-permute-start(f32[56,768]{1,0:T(8,128)} %get-tuple-element.24), channel_id=1, source_target_pairs={{0,8},{8,16},{16,24},{24,32},{32,40},{40,48},{48,56},{56,64},{64,7... | collective-permute-start | bytes 516104 | tf_op jit(solution)/shard_map/ppermute | solution.py:484
  2.8 3.9 %copy-start.10 = (f32[1,128]{1,0:T(1,128)S(1)}, f32[1,128]{1,0:T(1,128)}, u32[]{:S(2)}) copy-start(f32[1,128]{1,0:T(1,128)} %get-tuple-element.19.coef_row) | copy-start | bytes 1540
  2.8 8.1 %collective-permute-start.1 = (f32[56,768]{1,0:T(8,128)}, f32[56,768]{1,0:T(8,128)S(1)}, u32[]{:S(2)}, u32[]{:S(2)}) collective-permute-start(f32[56,768]{1,0:T(8,128)} %get-tuple-element.25), channel_id=1, source_target_pairs={{8,0},{16,8},{24,16},{32,24},{40,32},{48,40},{56,48},{64,56},{72,6... | collective-permute-start | bytes 516104 | tf_op jit(solution)/shard_map/ppermute | solution.py:485
  15.5 7.1 %copy-start.11 = (f32[96,96]{1,0:T(8,128)S(1)}, f32[96,96]{1,0:T(8,128)}, u32[]{:S(2)}) copy-start(f32[96,96]{1,0:T(8,128)} %param.17) | copy-start | bytes 110596
  15.5 23.6 %all-to-all-start = ((f32[8,8,3712]{2,1,0:T(8,128)}), f32[8,8,3712]{2,1,0:T(8,128)S(1)}, u32[]{:S(2)}, u32[]{:S(2)}) async-start(f32[8,8,3712]{2,1,0:T(8,128)} %get-tuple-element.28), calls=%async_computation | async-start | bytes 1900544 | tf_op jit(solution)/shard_map/all_to_all | solution.py:527
  23.2 0.8 %copy-start.9 = (f32[6,2048]{1,0:T(8,128)S(1)}, f32[6,2048]{1,0:T(8,128)}, u32[]{:S(2)}) copy-start(f32[6,2048]{1,0:T(8,128)} %lap.1) | copy-start | bytes 147460
  26.2 0.8 %copy-start.7 = (bf16[3,256,256]{2,1,0:T(8,128)(2,1)}, bf16[3,256,256]{2,1,0:T(8,128)(2,1)S(1)}, u32[]{:S(2)}) copy-start(bf16[3,256,256]{2,1,0:T(8,128)(2,1)S(1)} %get-tuple-element.35.refs_5_) | copy-start | bytes 1179652
  39.0 1.0 %copy-start.8 = (bf16[3,256,256]{2,1,0:T(8,128)(2,1)S(1)}, bf16[3,256,256]{2,1,0:T(8,128)(2,1)}, u32[]{:S(2)}) copy-start(bf16[3,256,256]{2,1,0:T(8,128)(2,1)} %copy-done.7) | copy-start | bytes 1179652

commit v5 on v4

--- a/solution.py
+++ b/solution.py
@@ -28,7 +28,8 @@
 MATRIX = 8
 HALF = WIDE // 2
 SENT = WIDE - LANES
-BANDS = 6
+BANDS = 5
+NEAR = SOLVED // (BANDS + 1)
 HALO_ROWS = 56
 COUPLING = 0.5
 
@@ -312,44 +313,49 @@
         send[j, :, SENT:] = rest_rs[:, HALF : 2 * HALF]
 
 
+def band_block(side, weight, col):
+    lane = lax.broadcasted_iota(jnp.int32, (1, LANES), 1)
+    slot = lax.broadcasted_iota(jnp.int32, (2 * LANES, LANES), 0)
+    cells = pl.ds(col, LANES)
+    dense = jnp.zeros((2 * LANES, LANES), f32)
+    for k in range(SIDES):
+        at = side[k : k + 1, cells] + (lane + NBR_REACH)
+        dense = dense + jnp.where(slot == at, weight[k : k + 1, cells], 0.0)
+    return split(dense)
+
+
 def band_kernel(left, right, nbr, lap, *refs):
-    *matrices, total, side, side_w = refs
-
-    own = lax.broadcasted_iota(jnp.int32, (1, CELLS), 1)
+    *matrices, near_side, near_weight, total, side, side_w = refs
     mid = slice(EDGE, EDGE + CELLS)
     for halo, cells in ((left, slice(0, EDGE)), (right, slice(EDGE + CELLS, WIDE))):
         side[0:4, cells] = halo[52:56, 0:EDGE].astype(jnp.int32)
         side[4:6, cells] = halo[52:54, 2 * EDGE :].astype(jnp.int32)
         side_w[0:4, cells] = halo[52:56, EDGE : 2 * EDGE]
         side_w[4:6, cells] = halo[54:56, 2 * EDGE :]
+    own = lax.broadcasted_iota(jnp.int32, (1, CELLS), 1)
     side[:, mid] = nbr[...] - NBR_REACH - own
     side_w[:, mid] = lap[...]
     total[...] = jnp.sum(side_w[...], axis=0, keepdims=True)
-    lane = lax.broadcasted_iota(jnp.int32, (1, LANES), 1)
-    slot = lax.broadcasted_iota(jnp.int32, (2 * LANES, LANES), 0)
-
-    per = SOLVED // BANDS
+    near_side[...] = side[:, LANES : (1 + NEAR) * LANES]
+    near_weight[...] = side_w[:, LANES : (1 + NEAR) * LANES]
     for part, matrix in enumerate(matrices):
 
         def block(b, carry):
-            cells = pl.ds(pl.multiple_of((part * per + b + 1) * LANES, LANES), LANES)
-            dense = jnp.zeros((2 * LANES, LANES), f32)
-            for k in range(SIDES):
-                at = side[k : k + 1, cells] + (lane + NBR_REACH)
-                dense = dense + jnp.where(slot == at, side_w[k : k + 1, cells], 0.0)
-            high, low = split(dense)
-            matrix[b, :, 0:LANES] = high
-            matrix[b, :, LANES:] = low
+            col = pl.multiple_of(((part + 1) * NEAR + b + 1) * LANES, LANES)
+            matrix[b, :, 0:LANES], matrix[b, :, LANES:] = band_block(side, side_w, col)
             return carry
 
-        lax.fori_loop(0, per, block, 0)
+        lax.fori_loop(0, NEAR, block, 0)
 
 
 def solve_kernel(
     got, total, to_first, to_second, from_rows, *refs
 ):
-    matrices, (out, x, rhs, scaled, parts, others, last) = refs[:BANDS], refs[BANDS:]
-    per = SOLVED // BANDS
+    near_side, near_weight, *matrices = refs[: BANDS + 2]
+    out, x, rhs, scaled, parts, others, last, held = refs[BANDS + 2 :]
+    for b in range(NEAR):
+        held[b, :, 0:LANES], held[b, :, LANES:] = band_block(near_side, near_weight, b * LANES)
+    matrices = [held, *matrices]
     modes = GROUPS * ROWS
     lane = lax.broadcasted_iota(jnp.int32, (1, LANES), 1)
     coef_row = jnp.sum(got[:, 4, SENT + HALF - LANES :], axis=0, keepdims=True)
@@ -399,7 +405,7 @@
 
     def swept(source, sweep, b):
         four = dot(
-            jnp.concatenate([source[b], source[b + 1]], axis=1), matrices[(b - 1) // per][(b - 1) % per]
+            jnp.concatenate([source[b], source[b + 1]], axis=1), matrices[(b - 1) // NEAR][(b - 1) % NEAR]
         )
         moved = four[:modes, :LANES] + (
             four[modes:, :LANES] + four[:modes, LANES:] + four[modes:, LANES:]
@@ -516,10 +522,11 @@
         packed, slabs, inner, inner_right, left, right, stencil_index, stencil_weight,
         side, edge_x, edge_y,
     )
-    bands = ((SOLVED // BANDS, 2 * LANES, 2 * LANES), bf16)
-    *matrices, total = call(
+    bands = ((NEAR, 2 * LANES, 2 * LANES), bf16)
+    near = (SIDES, NEAR * LANES)
+    *matrices, near_side, near_weight, total = call(
         band_kernel,
-        [bands] * BANDS + [((1, WIDE), f32)],
+        [bands] * BANDS + [(near, jnp.int32), (near, f32), ((1, WIDE), f32)],
         [pltpu.VMEM((SIDES, WIDE), jnp.int32), pltpu.VMEM((SIDES, WIDE), f32)],
         name="band",
         spaces=4 * "v",
@@ -536,10 +543,11 @@
         + [pltpu.VMEM((SOLVED + 2, 2 * modes, LANES), bf16)] * 2
         + [
             pltpu.VMEM((CELLS // (2 * LANES), 2 * modes, 2 * LANES), bf16),
+            pltpu.VMEM(*bands),
         ],
         name="solve",
-        spaces=(5 + BANDS) * "v",
-    )(got, total, *to_slabs, from_rows, *matrices)
+        spaces=(7 + BANDS) * "v",
+    )(got, total, *to_slabs, from_rows, near_side, near_weight, *matrices)
     return new_winds, new_height
 
 

time: 43.7 us -> 43 us (0.984)
  local copies, waits for them, and re-layouts: 3.09 us -> 1.34 us
  waiting for transfers between devices: 12.1 us -> 13.2 us
    unnamed x25 -> x21, local copies, waits for them, and re-layouts: 2.62 us -> 0.88 us
    all_to_all x1, waiting for transfers between devices: 12.1 us -> 13.2 us  [per_device(): got = lax.all_to_all(send, 'lev', split_axis=0, concat_axis=0, tiled=True)]
  transfers between devices with their start and end apart: 3 -> 3, of which waited for: 1 -> 1; matrix products, arithmetic and copies ran while one was open for 3% -> 3% of each run, Pallas kernels for 15% -> 14%
where the time goes in v5:
time: 43 us; the launch traced here: 42.7 us
  Pallas kernels  16.2 us (38%)
  waiting for transfers between devices  13.2 us (31%)
  starting transfers between devices  11 us (26%)
  local copies, waits for them, and re-layouts  1.34 us (3%)
  between operations  0.88 us (2%)
    all_to_all x1, waiting for transfers between devices, per_device(): got = lax.all_to_all(send, 'lev', split_axis=0, concat_axis=0, tiled=True)  13.2 us
    all_to_all x1, starting transfers between devices, per_device(): got = lax.all_to_all(send, 'lev', split_axis=0, concat_axis=0, tiled=True)  7.06 us
    pallas_call x1, Pallas kernels, per_device(): call(outer_kernel, [((2, ROWS, CELLS), f32), ((GROUPS, 8, SENT + HALF), f...  4.58 us
    pallas_call x1, Pallas kernels, per_device(): call(inner_kernel, [((40, CELLS), f32), ((tiles, 40, 2 * LANES), bf16), (...  4.17 us
    ppermute x1, starting transfers between devices, per_device(): lax.ppermute(head, 'patch', [((i + 1) % patches, i) for i in range(patche...  3.83 us
    pallas_call x1, Pallas kernels, per_device(): call(solve_kernel, [((ROWS, CELLS), f32)], [pltpu.VMEM((SOLVED + 1, modes...  3.7 us
    pallas_call x1, Pallas kernels, per_device(): call(halo_kernel, [halo, halo, ((1, LANES), f32)], buffers * 2 + [pltpu.S...  2 us
    pallas_call x1, Pallas kernels, per_device(): call(band_kernel, [bands] * BANDS + [(near, jnp.int32), (near, f32), ((1,...  1.79 us
  transfers between devices with their start and end apart: 3, of which 1 were waited for; matrix products, arithmetic and copies ran while one was open for 3% of the time, Pallas kernels for 14%

profile of v5, /device:TPU:128, one launch (start us, length us, event | category | flops | bytes accessed | tf_op | source)
XLA Modules:
  0.0 42.7 jit_solution(9528969990493743937)
XLA Ops:
  0.6 0.0 copy-start
  0.7 0.0 copy-start.1
  0.7 0.0 copy-start.2
  0.7 0.0 copy-start.3
  0.7 0.0 copy-start.4
  0.7 0.0 copy-start.5
  0.7 0.0 copy-start.6
  0.7 2.0 %halo.1 = (f32[56,768]{1,0:T(8,128)}, f32[56,768]{1,0:T(8,128)}, f32[1,128]{1,0:T(1,128)}) custom-call(s32[1]{0:T(128)} %bitcast.refs_0_, f32[12]{0:T(128)} %refs_1_.1, f32[3,12,2048]{2,1,0:T(8,128)} %fields.1, s32[12,1,2048]{2,1,0:T(1,128)} %index.3, f32[12,1,2048]{2,1,0:T(1,128)} %weight.3, s32[6,2048]{1,0:T(8,128)} %nbr.3, f32[6,2048]{1,0:T(8,128)} %lap.1, ...), custom_call_target="tpu_custom_call" | custom-call | tf_op jit(solution)/shard_map/halo/pallas_call | solution.py:479
  2.7 0.1 collective-permute-start
  2.8 0.0 copy-start.8
  2.8 3.8 %collective-permute-start.1 = (f32[56,768]{1,0:T(8,128)}, f32[56,768]{1,0:T(8,128)S(1)}, u32[]{:S(2)}, u32[]{:S(2)}) collective-permute-start(f32[56,768]{1,0:T(8,128)} %get-tuple-element.26), channel_id=1, source_target_pairs={{8,0},{16,8},{24,16},{32,24},{40,32},{48,40},{56,48},{64,56},{72,6... | collective-permute-start | bytes 516104 | tf_op jit(solution)/shard_map/ppermute | solution.py:491
  6.7 0.0 copy-done.1
  6.7 0.0 copy-done.2
  6.7 0.0 copy-done.3
  6.7 0.0 copy-done.4
  6.7 0.0 copy-done.5
  6.7 0.0 copy-done.6
  6.7 0.0 copy-done.8
  6.7 4.2 %inner.1 = (f32[40,2048]{1,0:T(8,128)S(1)}, bf16[16,40,256]{2,1,0:T(8,128)(2,1)S(1)}, f32[40,2048]{1,0:T(8,128)S(1)}, f32[12,768]{1,0:T(8,128)S(1)}, s32[6,2048]{1,0:T(8,128)S(1)}) custom-call(f32[3,12,2048]{2,1,0:T(8,128)S(1)} %copy-done.1, s32[12,1,2048]{2,1,0:T(1,128)S(1)} %copy-done.2, f32[12,1,2048]{2,1,0:T(1,128)S(1)} %copy-done.3, ...), custom_call_target="tpu_custom_call" | custom-call | tf_op jit(solution)/shard_map/inner/pallas_call | solution.py:493
  10.9 0.0 collective-permute-done.left
  10.9 0.0 collective-permute-done.1.right
  10.9 4.6 %outer.1 = (f32[2,12,2048]{2,1,0:T(8,128)S(1)}, f32[8,8,3712]{2,1,0:T(8,128)}) custom-call(f32[40,2048]{1,0:T(8,128)S(1)} %get-tuple-element.21.packed, bf16[16,40,256]{2,1,0:T(8,128)(2,1)S(1)} %get-tuple-element.22.own_slabs, f32[40,2048]{1,0:T(8,128)S(1)} %get-tuple-element.23.inner, f32[12,768]{1,0:T(8,128)S(1)} %get-tuple-element.24.inner_right, ...), custom_call_target="tpu_custom_call" | custom-call | tf_op jit(solution)/shard_map/outer/pallas_call | solution.py:506
  15.5 0.0 copy-start.9
  15.5 7.1 %all-to-all-start = ((f32[8,8,3712]{2,1,0:T(8,128)}), f32[8,8,3712]{2,1,0:T(8,128)S(1)}, u32[]{:S(2)}, u32[]{:S(2)}) async-start(f32[8,8,3712]{2,1,0:T(8,128)} %get-tuple-element.29), calls=%async_computation | async-start | bytes 1900544 | tf_op jit(solution)/shard_map/all_to_all | solution.py:534
  22.5 0.0 copy-done.9
  22.5 0.1 copy.13
  22.7 0.1 copy.17
  22.8 0.1 copy.14
  22.9 0.1 copy.15
  23.0 0.0 copy-done
  23.0 0.1 tile.10
  23.1 0.1 maximum_bitcast_fusion.1
  23.2 0.0 copy-start.7
  23.2 0.8 %copy.18 = f32[2,12,2048]{2,0,1:T(2,128)} copy(f32[2,12,2048]{2,1,0:T(8,128)S(1)} %get-tuple-element.40) | data formatting | bytes 393216
  24.0 0.0 copy-done.7
  24.0 1.8 %band.1 = (bf16[3,256,256]{2,1,0:T(8,128)(2,1)S(1)}, bf16[3,256,256]{2,1,0:T(8,128)(2,1)S(1)}, bf16[3,256,256]{2,1,0:T(8,128)(2,1)S(1)}, bf16[3,256,256]{2,1,0:T...) custom-call(f32[56,768]{1,0:T(8,128)S(1)} %collective-permute-done.l, ...), custom_call_target="tpu_custom_call" | custom-call | tf_op jit(solution)/shard_map/band/pallas_call | solution.py:527
  25.8 13.2 %all-to-all-done.got = f32[8,8,3712]{2,1,0:T(8,128)S(1)} async-done(((f32[8,8,3712]{2,1,0:T(8,128)}), f32[8,8,3712]{2,1,0:T(8,128)S(1)}, u32[]{:S(2)}, u32[]{:S(2)}) %all-to-all-start) | async-done | bytes 950304 | tf_op jit(solution)/shard_map/all_to_all | solution.py:534
  39.0 3.7 %solve.1 = f32[12,2048]{1,0:T(8,128)} custom-call(f32[8,8,3712]{2,1,0:T(8,128)S(1)} %all-to-all-done.got, f32[1,2560]{1,0:T(1,128)S(1)} %get-tuple-element.30.total, f32[96,128]{1,0:T(8,128)S(1)} %get-tuple-element.43.to_first, f32[96,128]{1,0:T(8,128)S(1)} %get-tuple-element.42.to_second, f32[16,192]{1,0:T(8,128)S(1)} %pad.14.from_rows, ...), custom_call_target="tpu_custom_call" | custom-call | tf_op jit(solution)/shard_map/solve/pallas_call | solution.py:539
  (7 shorter events, 0.1 us)
Async XLA Ops:
  0.6 22.3 %copy-start = (f32[96,96]{1,0:T(8,128)S(1)}, f32[96,96]{1,0:T(8,128)}, u32[]{:S(2)}) copy-start(f32[96,96]{1,0:T(8,128)} %param.18) | copy-start | bytes 110596
  0.7 6.0 %copy-start.1 = (f32[3,12,2048]{2,1,0:T(8,128)S(1)}, f32[3,12,2048]{2,1,0:T(8,128)}, u32[]{:S(2)}) copy-start(f32[3,12,2048]{2,1,0:T(8,128)} %fields.1) | copy-start | bytes 884740
  0.7 6.0 %copy-start.2 = (s32[12,1,2048]{2,1,0:T(1,128)S(1)}, s32[12,1,2048]{2,1,0:T(1,128)}, u32[]{:S(2)}) copy-start(s32[12,1,2048]{2,1,0:T(1,128)} %index.3) | copy-start | bytes 294916
  0.7 6.0 %copy-start.3 = (f32[12,1,2048]{2,1,0:T(1,128)S(1)}, f32[12,1,2048]{2,1,0:T(1,128)}, u32[]{:S(2)}) copy-start(f32[12,1,2048]{2,1,0:T(1,128)} %weight.3) | copy-start | bytes 294916
  0.7 6.0 %copy-start.4 = (f32[6,2048]{1,0:T(8,128)S(1)}, f32[6,2048]{1,0:T(8,128)}, u32[]{:S(2)}) copy-start(f32[6,2048]{1,0:T(8,128)} %ex.3) | copy-start | bytes 147460
  0.7 6.0 %copy-start.5 = (f32[6,2048]{1,0:T(8,128)S(1)}, f32[6,2048]{1,0:T(8,128)}, u32[]{:S(2)}) copy-start(f32[6,2048]{1,0:T(8,128)} %ey.3) | copy-start | bytes 147460
  0.7 6.0 %copy-start.6 = (s32[6,2048]{1,0:T(8,128)S(1)}, s32[6,2048]{1,0:T(8,128)}, u32[]{:S(2)}) copy-start(s32[6,2048]{1,0:T(8,128)} %nbr.3) | copy-start | bytes 147460
  2.7 8.2 %collective-permute-start = (f32[56,768]{1,0:T(8,128)}, f32[56,768]{1,0:T(8,128)S(1)}, u32[]{:S(2)}, u32[]{:S(2)}) collective-permute-start(f32[56,768]{1,0:T(8,128)} %get-tuple-element.25), channel_id=1, source_target_pairs={{0,8},{8,16},{16,24},{24,32},{32,40},{40,48},{48,56},{56,64},{64,7... | collective-permute-start | bytes 516104 | tf_op jit(solution)/shard_map/ppermute | solution.py:490
  2.8 3.9 %copy-start.8 = (f32[1,128]{1,0:T(1,128)S(1)}, f32[1,128]{1,0:T(1,128)}, u32[]{:S(2)}) copy-start(f32[1,128]{1,0:T(1,128)} %get-tuple-element.20.coef_row) | copy-start | bytes 1540
  2.8 8.1 %collective-permute-start.1 = (f32[56,768]{1,0:T(8,128)}, f32[56,768]{1,0:T(8,128)S(1)}, u32[]{:S(2)}, u32[]{:S(2)}) collective-permute-start(f32[56,768]{1,0:T(8,128)} %get-tuple-element.26), channel_id=1, source_target_pairs={{8,0},{16,8},{24,16},{32,24},{40,32},{48,40},{56,48},{64,56},{72,6... | collective-permute-start | bytes 516104 | tf_op jit(solution)/shard_map/ppermute | solution.py:491
  15.5 7.1 %copy-start.9 = (f32[96,96]{1,0:T(8,128)S(1)}, f32[96,96]{1,0:T(8,128)}, u32[]{:S(2)}) copy-start(f32[96,96]{1,0:T(8,128)} %param.17) | copy-start | bytes 110596
  15.5 23.6 %all-to-all-start = ((f32[8,8,3712]{2,1,0:T(8,128)}), f32[8,8,3712]{2,1,0:T(8,128)S(1)}, u32[]{:S(2)}, u32[]{:S(2)}) async-start(f32[8,8,3712]{2,1,0:T(8,128)} %get-tuple-element.29), calls=%async_computation | async-start | bytes 1900544 | tf_op jit(solution)/shard_map/all_to_all | solution.py:534
  23.2 0.8 %copy-start.7 = (f32[6,2048]{1,0:T(8,128)S(1)}, f32[6,2048]{1,0:T(8,128)}, u32[]{:S(2)}) copy-start(f32[6,2048]{1,0:T(8,128)} %lap.1) | copy-start | bytes 147460

commit v6 on v5

--- a/solution.py
+++ b/solution.py
@@ -51,7 +51,8 @@
 def halo_kernel(*refs):
     group, coef, *sources = refs[:9]
     head, tail, coef_row = refs[9:12]
-    buffers, coef_here, sems = refs[12:26], refs[26], refs[27]
+    buffers, coef_here, sems, staged = refs[12:26], refs[26], refs[27], refs[28:30]
+    sent = []
     copies = []
     for side, (field_col, col) in enumerate(((0, 0), (CELLS - FIELD_EDGE, CELLS - EDGE))):
         for n, source in enumerate(sources):
@@ -61,7 +62,8 @@
     copies.append(pltpu.make_async_copy(coef, coef_here, sems.at[14]))
     for copy in copies:
         copy.start()
-    for side, (out, col) in enumerate(((head, 0), (tail, CELLS - EDGE))):
+    for side, (far, col) in enumerate(((head, 0), (tail, CELLS - EDGE))):
+        out = staged[side]
         for copy in copies[7 * side : 7 * side + 7]:
             copy.wait()
         fields, index, weight, nbr, lap, ex, ey = buffers[7 * side : 7 * side + 7]
@@ -77,12 +79,16 @@
         out[46:52, 2 * EDGE :] = ey[...]
         out[52:54, 2 * EDGE :] = away[4:6]
         out[54:56, 2 * EDGE :] = lap[4:6]
+        sent.append(pltpu.make_async_copy(out, far, sems.at[15 + side]))
+        sent[side].start()
     copies[14].wait()
     lane = lax.broadcasted_iota(jnp.int32, (1, LANES), 1)
     row = jnp.zeros((1, LANES), f32)
     for k in range(ROWS):
         row = jnp.where(lane == group[0] * ROWS + k, coef_here[k], row)
     coef_row[...] = row
+    for copy in sent:
+        copy.wait()
 
 
 def split(v):
@@ -479,9 +485,11 @@
     head, tail, coef_row = call(
         halo_kernel,
         [halo, halo, ((1, LANES), f32)],
-        buffers * 2 + [pltpu.SMEM((ROWS,), f32), pltpu.SemaphoreType.DMA((15,))],
+        buffers * 2
+        + [pltpu.SMEM((ROWS,), f32), pltpu.SemaphoreType.DMA((17,)), pltpu.VMEM(*halo), pltpu.VMEM(*halo)],
         name="halo",
         spaces="s" + 8 * "h",
+        out_spaces="hhv",
         vmem=60,
     )(
         group[None], helm_coef, fields, stencil_index, stencil_weight, neighbours, lap_weight,

time: 43 us -> 43.5 us (1.012)
  Pallas kernels: 16.2 us -> 16.7 us
    pallas_call x1, Pallas kernels: 2 us -> 2.49 us  [per_device(): call(halo_kernel, [halo, halo, ((1, LANES), f32)], buffers * 2 + [pltpu.S...]
where the time goes in v6:
time: 43.5 us; the launch traced here: 43.2 us
  Pallas kernels  16.7 us (38%)
  waiting for transfers between devices  13.2 us (30%)
  starting transfers between devices  11 us (25%)
  local copies, waits for them, and re-layouts  1.34 us (3%)
  between operations  0.88 us (2%)
    all_to_all x1, waiting for transfers between devices, per_device(): got = lax.all_to_all(send, 'lev', split_axis=0, concat_axis=0, tiled=True)  13.2 us
    all_to_all x1, starting transfers between devices, per_device(): got = lax.all_to_all(send, 'lev', split_axis=0, concat_axis=0, tiled=True)  7.06 us
    pallas_call x1, Pallas kernels, per_device(): call(outer_kernel, [((2, ROWS, CELLS), f32), ((GROUPS, 8, SENT + HALF), f...  4.57 us
    pallas_call x1, Pallas kernels, per_device(): call(inner_kernel, [((40, CELLS), f32), ((tiles, 40, 2 * LANES), bf16), (...  4.16 us
    ppermute x1, starting transfers between devices, per_device(): lax.ppermute(head, 'patch', [((i + 1) % patches, i) for i in range(patche...  3.83 us
    pallas_call x1, Pallas kernels, per_device(): call(solve_kernel, [((ROWS, CELLS), f32)], [pltpu.VMEM((SOLVED + 1, modes...  3.7 us
    pallas_call x1, Pallas kernels, per_device(): call(halo_kernel, [halo, halo, ((1, LANES), f32)], buffers * 2 + [pltpu.S...  2.49 us
    pallas_call x1, Pallas kernels, per_device(): call(band_kernel, [bands] * BANDS + [(near, jnp.int32), (near, f32), ((1,...  1.79 us
  transfers between devices with their start and end apart: 3, of which 1 were waited for; matrix products, arithmetic and copies ran while one was open for 3% of the time, Pallas kernels for 14%

profile of v6, /device:TPU:128, one launch (start us, length us, event | category | flops | bytes accessed | tf_op | source)
XLA Modules:
  0.0 43.2 jit_solution(17036364309044541702)
XLA Ops:
  0.6 0.0 copy-start
  0.7 0.0 copy-start.1
  0.7 0.0 copy-start.2
  0.7 0.0 copy-start.3
  0.7 0.0 copy-start.4
  0.7 0.0 copy-start.5
  0.7 0.0 copy-start.6
  0.7 2.5 %halo.1 = (f32[56,768]{1,0:T(8,128)}, f32[56,768]{1,0:T(8,128)}, f32[1,128]{1,0:T(1,128)}) custom-call(s32[1]{0:T(128)} %bitcast.refs_0_, f32[12]{0:T(128)} %refs_1_.1, f32[3,12,2048]{2,1,0:T(8,128)} %fields.1, s32[12,1,2048]{2,1,0:T(1,128)} %index.3, f32[12,1,2048]{2,1,0:T(1,128)} %weight.3, s32[6,2048]{1,0:T(8,128)} %nbr.3, f32[6,2048]{1,0:T(8,128)} %lap.1, ...), custom_call_target="tpu_custom_call" | custom-call | tf_op jit(solution)/shard_map/halo/pallas_call | solution.py:485
  3.2 0.1 collective-permute-start
  3.3 0.0 copy-start.8
  3.3 3.8 %collective-permute-start.1 = (f32[56,768]{1,0:T(8,128)}, f32[56,768]{1,0:T(8,128)S(1)}, u32[]{:S(2)}, u32[]{:S(2)}) collective-permute-start(f32[56,768]{1,0:T(8,128)} %get-tuple-element.26), channel_id=1, source_target_pairs={{8,0},{16,8},{24,16},{32,24},{40,32},{48,40},{56,48},{64,56},{72,6... | collective-permute-start | bytes 516104 | tf_op jit(solution)/shard_map/ppermute | solution.py:499
  7.1 0.0 copy-done.1
  7.1 0.0 copy-done.2
  7.1 0.0 copy-done.3
  7.2 0.0 copy-done.4
  7.2 0.0 copy-done.5
  7.2 0.0 copy-done.6
  7.2 0.0 copy-done.8
  7.2 4.2 %inner.1 = (f32[40,2048]{1,0:T(8,128)S(1)}, bf16[16,40,256]{2,1,0:T(8,128)(2,1)S(1)}, f32[40,2048]{1,0:T(8,128)S(1)}, f32[12,768]{1,0:T(8,128)S(1)}, s32[6,2048]{1,0:T(8,128)S(1)}) custom-call(f32[3,12,2048]{2,1,0:T(8,128)S(1)} %copy-done.1, s32[12,1,2048]{2,1,0:T(1,128)S(1)} %copy-done.2, f32[12,1,2048]{2,1,0:T(1,128)S(1)} %copy-done.3, ...), custom_call_target="tpu_custom_call" | custom-call | tf_op jit(solution)/shard_map/inner/pallas_call | solution.py:501
  11.4 0.0 collective-permute-done.left
  11.4 0.0 collective-permute-done.1.right
  11.4 4.6 %outer.1 = (f32[2,12,2048]{2,1,0:T(8,128)S(1)}, f32[8,8,3712]{2,1,0:T(8,128)}) custom-call(f32[40,2048]{1,0:T(8,128)S(1)} %get-tuple-element.21.packed, bf16[16,40,256]{2,1,0:T(8,128)(2,1)S(1)} %get-tuple-element.22.own_slabs, f32[40,2048]{1,0:T(8,128)S(1)} %get-tuple-element.23.inner, f32[12,768]{1,0:T(8,128)S(1)} %get-tuple-element.24.inner_right, ...), custom_call_target="tpu_custom_call" | custom-call | tf_op jit(solution)/shard_map/outer/pallas_call | solution.py:514
  15.9 0.0 copy-start.9
  15.9 7.1 %all-to-all-start = ((f32[8,8,3712]{2,1,0:T(8,128)}), f32[8,8,3712]{2,1,0:T(8,128)S(1)}, u32[]{:S(2)}, u32[]{:S(2)}) async-start(f32[8,8,3712]{2,1,0:T(8,128)} %get-tuple-element.29), calls=%async_computation | async-start | bytes 1900544 | tf_op jit(solution)/shard_map/all_to_all | solution.py:542
  23.0 0.0 copy-done.9
  23.0 0.1 copy.13
  23.1 0.1 copy.17
  23.2 0.1 copy.14
  23.3 0.1 copy.15
  23.4 0.0 copy-done
  23.5 0.1 tile.10
  23.6 0.1 maximum_bitcast_fusion.1
  23.7 0.0 copy-start.7
  23.7 0.8 %copy.18 = f32[2,12,2048]{2,0,1:T(2,128)} copy(f32[2,12,2048]{2,1,0:T(8,128)S(1)} %get-tuple-element.40) | data formatting | bytes 393216
  24.5 0.0 copy-done.7
  24.5 1.8 %band.1 = (bf16[3,256,256]{2,1,0:T(8,128)(2,1)S(1)}, bf16[3,256,256]{2,1,0:T(8,128)(2,1)S(1)}, bf16[3,256,256]{2,1,0:T(8,128)(2,1)S(1)}, bf16[3,256,256]{2,1,0:T...) custom-call(f32[56,768]{1,0:T(8,128)S(1)} %collective-permute-done.l, ...), custom_call_target="tpu_custom_call" | custom-call | tf_op jit(solution)/shard_map/band/pallas_call | solution.py:535
  26.3 13.2 %all-to-all-done.got = f32[8,8,3712]{2,1,0:T(8,128)S(1)} async-done(((f32[8,8,3712]{2,1,0:T(8,128)}), f32[8,8,3712]{2,1,0:T(8,128)S(1)}, u32[]{:S(2)}, u32[]{:S(2)}) %all-to-all-start) | async-done | bytes 950304 | tf_op jit(solution)/shard_map/all_to_all | solution.py:542
  39.5 3.7 %solve.1 = f32[12,2048]{1,0:T(8,128)} custom-call(f32[8,8,3712]{2,1,0:T(8,128)S(1)} %all-to-all-done.got, f32[1,2560]{1,0:T(1,128)S(1)} %get-tuple-element.30.total, f32[96,128]{1,0:T(8,128)S(1)} %get-tuple-element.43.to_first, f32[96,128]{1,0:T(8,128)S(1)} %get-tuple-element.42.to_second, f32[16,192]{1,0:T(8,128)S(1)} %pad.14.from_rows, ...), custom_call_target="tpu_custom_call" | custom-call | tf_op jit(solution)/shard_map/solve/pallas_call | solution.py:547
  (7 shorter events, 0.1 us)
Async XLA Ops:
  0.6 22.8 %copy-start = (f32[96,96]{1,0:T(8,128)S(1)}, f32[96,96]{1,0:T(8,128)}, u32[]{:S(2)}) copy-start(f32[96,96]{1,0:T(8,128)} %param.18) | copy-start | bytes 110596
  0.7 6.5 %copy-start.1 = (f32[3,12,2048]{2,1,0:T(8,128)S(1)}, f32[3,12,2048]{2,1,0:T(8,128)}, u32[]{:S(2)}) copy-start(f32[3,12,2048]{2,1,0:T(8,128)} %fields.1) | copy-start | bytes 884740
  0.7 6.5 %copy-start.2 = (s32[12,1,2048]{2,1,0:T(1,128)S(1)}, s32[12,1,2048]{2,1,0:T(1,128)}, u32[]{:S(2)}) copy-start(s32[12,1,2048]{2,1,0:T(1,128)} %index.3) | copy-start | bytes 294916
  0.7 6.5 %copy-start.3 = (f32[12,1,2048]{2,1,0:T(1,128)S(1)}, f32[12,1,2048]{2,1,0:T(1,128)}, u32[]{:S(2)}) copy-start(f32[12,1,2048]{2,1,0:T(1,128)} %weight.3) | copy-start | bytes 294916
  0.7 6.5 %copy-start.4 = (f32[6,2048]{1,0:T(8,128)S(1)}, f32[6,2048]{1,0:T(8,128)}, u32[]{:S(2)}) copy-start(f32[6,2048]{1,0:T(8,128)} %ex.3) | copy-start | bytes 147460
  0.7 6.5 %copy-start.5 = (f32[6,2048]{1,0:T(8,128)S(1)}, f32[6,2048]{1,0:T(8,128)}, u32[]{:S(2)}) copy-start(f32[6,2048]{1,0:T(8,128)} %ey.3) | copy-start | bytes 147460
  0.7 6.5 %copy-start.6 = (s32[6,2048]{1,0:T(8,128)S(1)}, s32[6,2048]{1,0:T(8,128)}, u32[]{:S(2)}) copy-start(s32[6,2048]{1,0:T(8,128)} %nbr.3) | copy-start | bytes 147460
  3.2 8.2 %collective-permute-start = (f32[56,768]{1,0:T(8,128)}, f32[56,768]{1,0:T(8,128)S(1)}, u32[]{:S(2)}, u32[]{:S(2)}) collective-permute-start(f32[56,768]{1,0:T(8,128)} %get-tuple-element.25), channel_id=1, source_target_pairs={{0,8},{8,16},{16,24},{24,32},{32,40},{40,48},{48,56},{56,64},{64,7... | collective-permute-start | bytes 516104 | tf_op jit(solution)/shard_map/ppermute | solution.py:498
  3.3 3.9 %copy-start.8 = (f32[1,128]{1,0:T(1,128)S(1)}, f32[1,128]{1,0:T(1,128)}, u32[]{:S(2)}) copy-start(f32[1,128]{1,0:T(1,128)} %get-tuple-element.20.coef_row) | copy-start | bytes 1540
  3.3 8.1 %collective-permute-start.1 = (f32[56,768]{1,0:T(8,128)}, f32[56,768]{1,0:T(8,128)S(1)}, u32[]{:S(2)}, u32[]{:S(2)}) collective-permute-start(f32[56,768]{1,0:T(8,128)} %get-tuple-element.26), channel_id=1, source_target_pairs={{8,0},{16,8},{24,16},{32,24},{40,32},{48,40},{56,48},{64,56},{72,6... | collective-permute-start | bytes 516104 | tf_op jit(solution)/shard_map/ppermute | solution.py:499
  15.9 7.1 %copy-start.9 = (f32[96,96]{1,0:T(8,128)S(1)}, f32[96,96]{1,0:T(8,128)}, u32[]{:S(2)}) copy-start(f32[96,96]{1,0:T(8,128)} %param.17) | copy-start | bytes 110596
  15.9 23.6 %all-to-all-start = ((f32[8,8,3712]{2,1,0:T(8,128)}), f32[8,8,3712]{2,1,0:T(8,128)S(1)}, u32[]{:S(2)}, u32[]{:S(2)}) async-start(f32[8,8,3712]{2,1,0:T(8,128)} %get-tuple-element.29), calls=%async_computation | async-start | bytes 1900544 | tf_op jit(solution)/shard_map/all_to_all | solution.py:542
  23.7 0.8 %copy-start.7 = (f32[6,2048]{1,0:T(8,128)S(1)}, f32[6,2048]{1,0:T(8,128)}, u32[]{:S(2)}) copy-start(f32[6,2048]{1,0:T(8,128)} %lap.1) | copy-start | bytes 147460
